TPU v7x, 128 devices: a whole 4x4x4 slice. The times are simulated.
128 devices in a mesh: grp: 64 (over z, y, x), tp: 2 (over core).
Axes of the slice: x: 4, y: 4, z: 4, core: 2. Of those that a mesh axis runs over, the one named last changes fastest.
Arguments:
- hidden_in: bfloat16 [4096, 2, 2560], P('grp'), may hold values from -6 to 6
- prompt_len: int32 [48], replicated, may hold values from 1 to 32768, as said below
- slot_req: int32 [64], replicated, may hold values from 0 to 47, as said below
- sample_req: int32 [4096, 1], P('grp'), may hold values from 0 to 47; in each aligned block of 64 rows (0 to 63, 64 to 127, ...) at most 2 rows name the same one
- tail_len: int32 [4096], P('grp'), may hold values from 0 to 256
- slot_kv: bfloat16 [64, 8, 2, 80, 2048], P('grp', 'tp'), may hold values from -60 to 60
- tail_kv: bfloat16 [4096, 8, 2, 80, 256], P('grp', 'tp'), may hold values from -6 to 6
- attn_gain: float32 [2560], replicated, may hold values from 0.5 to 1.5
- wqkv: bfloat16 [2560, 3840], P(None, 'tp'), may hold values from -0.25 to 0.25
- wo: bfloat16 [2560, 2560], P('tp'), may hold values from -0.125 to 0.125
- out_gain: float32 [2560], replicated, may hold values from 0.5 to 1.5
- score_w: float32 [2560], replicated, may hold values from -0.125 to 0.125
Outputs:
- hidden_out: float32 [4096, 2, 2560], P('grp', None, 'tp')
- row_score: float32 [4096, 2], P('grp')
Inputs may be any that keep to these rules, and one draw needn't show every extreme that they name: `prompt_len`: exactly 16 prompts are longer than 2048 tokens. `slot_req`: a prompt of at most 2048 tokens owns one slot, a longer one two. `sample_req`: among the samples of one index of grp no prompt appears more than 2 times.
All inputs are finite; a program needn't handle non-finite values.
Results may differ from a plain program's by a relative error of at most 0.012.
Values may be sent and summed in bfloat16 or wider, within the bound.
A program may use at most 192 MiB of HBM per device.

v0:
```python
import jax
import jax.numpy as jnp
from jax import lax
from jax.sharding import PartitionSpec as P

W = 4096


epsilon = 1e-05
rope_base = 10000.0
neg_large = -1e30
key_block = 512


def rope_pair(positions, head_dim):
    half_dim = head_dim // 2
    frequency = rope_base ** (-jnp.arange(half_dim, dtype=jnp.float32) / half_dim)
    angles = positions.astype(jnp.float32)[..., None] * frequency
    angles = jnp.concatenate([angles, angles], axis=-1)
    return (jnp.cos(angles), jnp.sin(angles))


def rotate(vectors, cosine, sine):
    half_dim = vectors.shape[-1] // 2
    turned = jnp.concatenate([-vectors[..., half_dim:], vectors[..., :half_dim]], axis=-1)
    return vectors * cosine + turned * sine


def slot_attention(got_queries, got_tails, slot_kv, prompt_len, slot_req):
    groups = got_queries.shape[0]
    item_count = got_queries.shape[1]
    kv_heads = slot_kv.shape[1]
    head_dim = slot_kv.shape[3]
    slot_len = slot_kv.shape[4]
    per_kv = got_queries.shape[2] // (2 * kv_heads * head_dim)
    me_index = lax.axis_index("grp")
    my_request = slot_req[me_index]
    all_slots = jnp.arange(slot_req.shape[0], dtype=jnp.int32)
    my_part = jnp.sum(((slot_req == my_request) & (all_slots < me_index)).astype(jnp.int32))
    length = prompt_len[my_request]
    cached = jnp.minimum(length, W)
    live_count = jnp.clip(cached - my_part * slot_len, 0, slot_len)
    first_pos = length - cached + my_part * slot_len
    query_pos = length + got_tails[:, :, None] + jnp.arange(2, dtype=jnp.int32)[None, None, :]
    lowest = query_pos - W + 1
    lowest = jnp.broadcast_to(lowest[..., None], (groups, item_count, 2, per_kv)).reshape(-1)
    queries = got_queries.reshape(groups, item_count, 2, kv_heads, per_kv, head_dim)
    queries = queries.transpose(3, 0, 1, 2, 4, 5).reshape(kv_heads, -1, head_dim)
    row_count = queries.shape[1]
    slot_keys = slot_kv[0, :, 0]
    slot_values = slot_kv[0, :, 1]
    block_width = min(key_block, slot_len)
    score_scale = head_dim ** (-0.5)

    def key_step(block_num, carry):
        run_max, run_sum, run_acc = carry
        block_start = block_num * block_width
        key_part = lax.dynamic_slice_in_dim(slot_keys, block_start, block_width, 2)
        value_part = lax.dynamic_slice_in_dim(slot_values, block_start, block_width, 2)
        scores = (
            jnp.einsum("krh,khn->krn", queries, key_part, preferred_element_type=jnp.float32)
            * score_scale
        )
        offsets = block_start + jnp.arange(block_width, dtype=jnp.int32)
        usable = (offsets < live_count)[None, :] & (
            (first_pos + offsets)[None, :] >= lowest[:, None]
        )
        usable = usable[None]
        scores = jnp.where(usable, scores, neg_large)
        new_max = jnp.maximum(run_max, jnp.max(scores, axis=-1))
        weights = jnp.where(usable, jnp.exp(scores - new_max[..., None]), 0.0)
        factor = jnp.exp(run_max - new_max)
        run_sum = run_sum * factor + jnp.sum(weights, axis=-1)
        run_acc = run_acc * factor[..., None] + jnp.einsum(
            "krn,khn->krh",
            weights.astype(jnp.bfloat16),
            value_part,
            preferred_element_type=jnp.float32,
        )
        return (new_max, run_sum, run_acc)

    blocks = (live_count + block_width - 1) // block_width
    initial = (
        jnp.full((kv_heads, row_count), neg_large, jnp.float32),
        jnp.zeros((kv_heads, row_count), jnp.float32),
        jnp.zeros((kv_heads, row_count, head_dim), jnp.float32),
    )
    run_max, run_sum, run_acc = lax.fori_loop(0, blocks, key_step, initial)
    part_max = (
        run_max.reshape(kv_heads, groups, item_count, 2, per_kv)
        .transpose(1, 2, 3, 0, 4)
        .reshape(groups, item_count, -1)
    )
    part_sum = (
        run_sum.reshape(kv_heads, groups, item_count, 2, per_kv)
        .transpose(1, 2, 3, 0, 4)
        .reshape(groups, item_count, -1)
    )
    part_acc = (
        run_acc.reshape(kv_heads, groups, item_count, 2, per_kv, head_dim)
        .transpose(1, 2, 3, 0, 4, 5)
        .reshape(groups, item_count, -1)
    )
    return (part_max, part_sum, part_acc)


def local(
    hidden_in,
    prompt_len,
    slot_req,
    sample_req,
    tail_len,
    slot_kv,
    tail_kv,
    attn_gain,
    wqkv,
    wo,
    out_gain,
    score_w,
):
    samples = hidden_in.shape[0]
    model_dim = hidden_in.shape[2]
    kv_heads = slot_kv.shape[1]
    head_dim = slot_kv.shape[3]
    tail_max = tail_kv.shape[4]
    per_kv = wqkv.shape[1] // (kv_heads * head_dim) - 2
    groups = lax.axis_size("grp")
    requests = prompt_len.shape[0]
    capacity = max(2, -(-samples // requests))
    score_scale = head_dim ** (-0.5)
    flat_in = hidden_in.reshape(samples * 2, model_dim).astype(jnp.float32)
    normed = (
        flat_in
        * lax.rsqrt(jnp.mean(flat_in * flat_in, axis=-1, keepdims=True) + epsilon)
        * attn_gain
    ).astype(jnp.bfloat16)
    projected = jnp.dot(normed, wqkv, preferred_element_type=jnp.float32).reshape(
        samples, 2, kv_heads, per_kv + 2, head_dim
    )
    my_reqs = sample_req[:, 0]
    positions = (
        prompt_len[my_reqs][:, None] + tail_len[:, None] + jnp.arange(2, dtype=jnp.int32)[None, :]
    )
    cosine, sine = rope_pair(positions, head_dim)
    query_new = rotate(
        projected[:, :, :, :per_kv], cosine[:, :, None, None, :], sine[:, :, None, None, :]
    ).astype(jnp.bfloat16)
    key_new = rotate(projected[:, :, :, per_kv], cosine[:, :, None, :], sine[:, :, None, :]).astype(
        jnp.bfloat16
    )
    value_new = projected[:, :, :, per_kv + 1].astype(jnp.bfloat16)
    sample_ids = jnp.arange(samples, dtype=jnp.int32)
    same_req = my_reqs[:, None] == my_reqs[None, :]
    ranks = jnp.sum(
        (same_req & (sample_ids[:, None] > sample_ids[None, :])).astype(jnp.int32), axis=1
    )
    query_flat = query_new.reshape(samples, -1)
    rank_slots = jnp.arange(capacity, dtype=jnp.int32)
    match = (my_reqs[None, None, :] == slot_req[:, None, None]) & (
        ranks[None, None, :] == rank_slots[None, :, None]
    )
    found = jnp.any(match, axis=-1)
    source = jnp.sum(jnp.where(match, sample_ids[None, None, :], 0), axis=-1)
    send_queries = jnp.where(
        found[..., None], jnp.take(query_flat, source, axis=0), jnp.zeros((), jnp.bfloat16)
    )
    send_tails = jnp.where(found, jnp.take(tail_len, source, axis=0), 0)
    part_max, part_sum, part_acc = slot_attention(
        lax.all_to_all(send_queries, "grp", split_axis=0, concat_axis=0, tiled=True),
        lax.all_to_all(send_tails, "grp", split_axis=0, concat_axis=0, tiled=True),
        slot_kv,
        prompt_len,
        slot_req,
    )
    back_max = lax.all_to_all(part_max, "grp", split_axis=0, concat_axis=0, tiled=True)
    back_sum = lax.all_to_all(part_sum, "grp", split_axis=0, concat_axis=0, tiled=True)
    back_acc = lax.all_to_all(part_acc, "grp", split_axis=0, concat_axis=0, tiled=True)
    slot_ids = jnp.arange(groups, dtype=jnp.int32)
    owns = slot_req[None, :] == jnp.arange(requests, dtype=jnp.int32)[:, None]
    first_slot = jnp.min(jnp.where(owns, slot_ids[None, :], groups), axis=1)
    second_slot = jnp.max(jnp.where(owns, slot_ids[None, :], -1), axis=1)
    index_one = first_slot[my_reqs] * capacity + ranks
    index_two = second_slot[my_reqs] * capacity + ranks
    split_req = (first_slot != second_slot)[my_reqs]
    flat_max = back_max.reshape(groups * capacity, 2, kv_heads, per_kv)
    flat_sum = back_sum.reshape(groups * capacity, 2, kv_heads, per_kv)
    flat_acc = back_acc.reshape(groups * capacity, 2, kv_heads, per_kv, head_dim)
    split_mask = split_req[:, None, None, None]
    max_one = jnp.take(flat_max, index_one, axis=0)
    sum_one = jnp.take(flat_sum, index_one, axis=0)
    acc_one = jnp.take(flat_acc, index_one, axis=0)
    max_two = jnp.where(split_mask, jnp.take(flat_max, index_two, axis=0), neg_large)
    sum_two = jnp.where(split_mask, jnp.take(flat_sum, index_two, axis=0), 0.0)
    acc_two = jnp.where(split_mask[..., None], jnp.take(flat_acc, index_two, axis=0), 0.0)
    tail_keys = tail_kv[:, :, 0]
    tail_values = tail_kv[:, :, 1]
    tail_scores = (
        jnp.einsum("stkjh,skhn->stkjn", query_new, tail_keys, preferred_element_type=jnp.float32)
        * score_scale
    )
    tail_ok = (jnp.arange(tail_max, dtype=jnp.int32)[None, :] < tail_len[:, None])[
        :, None, None, None, :
    ]
    own_scores = (
        jnp.einsum("stkjh,sukh->stkju", query_new, key_new, preferred_element_type=jnp.float32)
        * score_scale
    )
    token_ids = jnp.arange(2, dtype=jnp.int32)
    own_ok = (token_ids[None, :] <= token_ids[:, None])[None, :, None, None, :]
    tail_scores = jnp.where(tail_ok, tail_scores, neg_large)
    own_scores = jnp.where(own_ok, own_scores, neg_large)
    home_max = jnp.maximum(jnp.max(tail_scores, axis=-1), jnp.max(own_scores, axis=-1))
    tail_weights = jnp.where(tail_ok, jnp.exp(tail_scores - home_max[..., None]), 0.0)
    own_weights = jnp.where(own_ok, jnp.exp(own_scores - home_max[..., None]), 0.0)
    home_sum = jnp.sum(tail_weights, axis=-1) + jnp.sum(own_weights, axis=-1)
    home_acc = jnp.einsum(
        "stkjn,skhn->stkjh",
        tail_weights.astype(jnp.bfloat16),
        tail_values,
        preferred_element_type=jnp.float32,
    )
    home_acc = home_acc + jnp.einsum(
        "stkju,sukh->stkjh",
        own_weights.astype(jnp.bfloat16),
        value_new,
        preferred_element_type=jnp.float32,
    )
    highest = jnp.maximum(home_max, jnp.maximum(max_one, max_two))
    weight_home = jnp.exp(home_max - highest)
    weight_one = jnp.exp(max_one - highest)
    weight_two = jnp.exp(max_two - highest)
    total_sum = home_sum * weight_home + sum_one * weight_one + sum_two * weight_two
    total_acc = (
        home_acc * weight_home[..., None]
        + acc_one * weight_one[..., None]
        + acc_two * weight_two[..., None]
    )
    attention = (total_acc / total_sum[..., None]).astype(jnp.bfloat16).reshape(samples * 2, -1)
    mixed = jnp.dot(attention, wo, preferred_element_type=jnp.float32)
    share_width = model_dim // lax.axis_size("tp")
    share_start = lax.axis_index("tp") * share_width
    head_total = lax.psum(mixed, "tp")
    residual = flat_in + head_total
    mean_square = jnp.mean(residual * residual, axis=-1)
    row_score = jnp.sum(residual * out_gain * score_w, axis=-1) * lax.rsqrt(mean_square + epsilon)
    residual_share = lax.dynamic_slice_in_dim(residual, share_start, share_width, 1)
    hidden_out = residual_share.reshape(samples, 2, share_width)
    return (hidden_out, row_score.reshape(samples, 2))


def solution(mesh):
    in_specs = (
        P("grp", None, None),
        P(),
        P(),
        P("grp", None),
        P("grp"),
        P("grp", "tp", None, None, None),
        P("grp", "tp", None, None, None),
        P(),
        P(None, "tp"),
        P("tp", None),
        P(),
        P(),
    )
    out_specs = (P("grp", None, "tp"), P("grp", None))
    return jax.shard_map(local, mesh=mesh, in_specs=in_specs, out_specs=out_specs, check_vma=False)
```

profile of v0, /device:TPU:1, one launch (start us, length us, event | category | flops | bytes accessed | tf_op | source)
XLA Modules:
  0.0 291.3 jit_solution(12044822590368251435)
XLA Ops:
  12.1 12.2 %all-to-all-start = ((s32[64,1,2]{2,1,0:T(1,128)}), s32[64,1,2]{2,1,0:T(1,128)}, u32[]{:S(2)}, u32[]{:S(2)}) async-start(s32[64,1,2]{2,1,0:T(1,128)} %copy.260), calls=%async_computation | async-start | bytes 65536 | tf_op jit(solution)/shard_map/all_to_all | solution.py:170
  31.6 13.6 %copy.239 = bf16[2560,1920]{0,1:T(8,128)(2,1)} copy(bf16[2560,1920]{1,0:T(8,128)(2,1)} %param.26) | data formatting | bytes 19660800 | tf_op args[8]
  46.7 7.1 %fusion.49 = f32[64,2,4,6,80]{4,0,3,2,1:T(8,128)S(1)} fusion(bf16[4,6,80,2560,1]{3,2,1,0,4:T(8,128)(2,1)} %bitcast.128, bf16[64,2,2560,1,1]{2,1,0,4,3:T(2,128)(2,1)S(1)} %fusion.48), kind=kOutput, calls=%fused_computation.78 | convolution fusion | flops 1258291200 | bytes 11468800 | tf_op jit(solution)/shard_map/dot_general | solution.py:137
  58.3 1.7 fusion.41
  64.8 3.1 %slice_bitcast_fusion = (bf16[4,80,2048]{2,1,0:T(8,128)(2,1)}, bf16[4,80,2048]{2,1,0:T(8,128)(2,1)S(1)}) fusion(bf16[1,4,2,80,2048]{4,3,2,1,0:T(8,128)(2,1)} %param.23), kind=kLoop, calls=%fused_computation.54 | loop fusion | bytes 5242880 | tf_op jit(solution)/shard_map/squeeze | solution.py:51
  68.9 6.4 %fusion.74 = (f32[64,2,4,4]{3,1,2,0:T(2,128)}, f32[64,2,4,4,2]{3,4,1,2,0:T(2,128)}) fusion(bf16[64,2,4,4,80]{4,0,3,2,1:T(8,128)(2,1)S(1)} %copy-done.10, bf16[64,2,4,80,1]{3,0,2,1,4:T(8,128)(2,1)S(1)} %fusion.56, pred[2,2]{1,0:T(4,128)(4,1)S(1)} %copy-done.36), kind=kOutput, calls=%fused_computation.151 | convolution fusion | flops 665600 | bytes 434180 | tf_op jit(solution)/shard_map/stkjh,sukh->stkju/dot_general | solution.py:205
  75.3 1.7 copy.246
  77.0 8.4 %bitcast_reduce_fusion = (f32[64,2,4,4]{3,1,2,0:T(2,128)}, f32[64,4,2,4,256]{4,3,2,1,0:T(4,128)}) fusion(pred[64,256]{1,0:T(8,128)(4,1)} %iota_compare_fusion, bf16[64,4,2,80,256]{4,3,2,1,0:T(8,128)(2,1)} %param.24, bf16[64,2,4,4,80]{4,0,3,2,1:T(8,128)(2,1)} %copy-done.9), kind=kOutput, calls=%fused_computation.42 | convolution fusion | flops 85456896 | bytes 13131776 | tf_op jit(solution)/shard_map/stkjh,skhn->stkjn/dot_general | solution.py:198
  85.3 1.7 copy.245
  88.4 1.6 copy.247
  89.9 4.5 %fusion.46 = f32[64,2,4,4]{3,1,2,0:T(2,128)} fusion(f32[64,2,4,4]{3,1,2,0:T(2,128)} %copy.247, f32[64,4,2,4,256]{4,3,2,1,0:T(4,128)} %get-tuple-element.223, pred[64,256]{1,0:T(8,128)(4,1)} %iota_compare_fusion), kind=kLoop, calls=%fused_computation.76 | loop fusion | flops 2619392 | bytes 2129920 | tf_op jit(solution)/shard_map/reduce_sum | solution.py:215
  94.4 1.8 broadcast_select_fusion.1
  96.2 1.4 gather_fusion.5
  97.6 1.4 gather_fusion.3
  99.1 9.9 %all-to-all-start.1 = ((bf16[64,2,2560]{2,1,0:T(2,128)(2,1)}), bf16[64,2,2560]{2,1,0:T(2,128)(2,1)}, u32[]{:S(2)}, u32[]{:S(2)}) async-start(bf16[64,2,2560]{2,1,0:T(2,128)(2,1)} %broadcast_select_fusion.1), calls=%async_computation.1 | async-start | bytes 1310720 | tf_op jit(solution)/shard_map/all_to_all | solution.py:169
  111.4 10.5 %all-to-all-done.1 = bf16[64,2,2560]{2,1,0:T(2,128)(2,1)} async-done(((bf16[64,2,2560]{2,1,0:T(2,128)(2,1)}), bf16[64,2,2560]{2,1,0:T(2,128)(2,1)}, u32[]{:S(2)}, u32[]{:S(2)}) %all-to-all-start.1) | async-done | bytes 655392 | tf_op jit(solution)/shard_map/all_to_all | solution.py:169
  121.9 2.0 copy.256
  123.9 3.6 %reshape.391 = bf16[64,2,2,4,4,80]{5,4,3,2,0,1:T(4,128)(2,1)S(1)} reshape(bf16[64,2,2560]{2,0,1:T(8,128)(2,1)} %copy.256) | data formatting | bytes 1310720 | tf_op jit(solution)/shard_map/reshape | solution.py:47
  128.8 1.5 copy.263
  131.5 39.8 %while.15 = (s32[]{:T(128)}, f32[4,1024]{1,0:T(4,128)S(1)}, f32[4,1024]{1,0:T(4,128)S(1)}, f32[4,1024,80]{1,2,0:T(8,128)}, s32[]{:T(128)}, /*index=5*/s32[]{:T(1...) while((s32[]{:T(128)}, f32[4,1024]{1,0:T(4,128)S(1)}, ...), condition=%wide.region_10.11_spmd.clone, body=%wide.region_7.10_spmd.clone.sunk | while | flops 700065792 | bytes 41965836 | solution.py:88
  132.4 1.8 fusion.93
  134.2 2.1 fusion.94
  136.4 4.0 %fusion.95 = f32[4,1024,80]{1,2,0:T(8,128)S(1)} fusion(f32[4,512,1024]{2,1,0:T(8,128)S(1)} %get-tuple-element.301, f32[4,1024]{1,0:T(4,128)S(1)} %max.46, pred[1024,512]{0,1:T(8,128)(4,1)S(1)} %compare_and_fusion.5, f32[4,1024,80]{1,2,0:T(8,128)S(1)} %copy-done.3, f32[4,1024]{1,0:T(4,128)S(1)} %get-tuple-element.303, ...), kind=kOutput, calls=%fused_computation.21.clone.1 | convolution fusion | flops 346685440 | bytes 11894788 | tf_op jit(solution)/shard_map/while/body/krn,khn->krh/dot_general | solution.py:74
  142.2 1.8 fusion.93
  144.1 2.1 fusion.94
  146.2 4.0 %fusion.95 = f32[4,1024,80]{1,2,0:T(8,128)S(1)} fusion(f32[4,512,1024]{2,1,0:T(8,128)S(1)} %get-tuple-element.301, f32[4,1024]{1,0:T(4,128)S(1)} %max.46, pred[1024,512]{0,1:T(8,128)(4,1)S(1)} %compare_and_fusion.5, f32[4,1024,80]{1,2,0:T(8,128)S(1)} %copy-done.3, f32[4,1024]{1,0:T(4,128)S(1)} %get-tuple-element.303, ...), kind=kOutput, calls=%fused_computation.21.clone.1 | convolution fusion | flops 346685440 | bytes 11894788 | tf_op jit(solution)/shard_map/while/body/krn,khn->krh/dot_general | solution.py:74
  152.1 1.8 fusion.93
  153.9 2.1 fusion.94
  156.1 4.0 %fusion.95 = f32[4,1024,80]{1,2,0:T(8,128)S(1)} fusion(f32[4,512,1024]{2,1,0:T(8,128)S(1)} %get-tuple-element.301, f32[4,1024]{1,0:T(4,128)S(1)} %max.46, pred[1024,512]{0,1:T(8,128)(4,1)S(1)} %compare_and_fusion.5, f32[4,1024,80]{1,2,0:T(8,128)S(1)} %copy-done.3, f32[4,1024]{1,0:T(4,128)S(1)} %get-tuple-element.303, ...), kind=kOutput, calls=%fused_computation.21.clone.1 | convolution fusion | flops 346685440 | bytes 11894788 | tf_op jit(solution)/shard_map/while/body/krn,khn->krh/dot_general | solution.py:74
  161.9 1.8 fusion.93
  163.7 2.1 fusion.94
  165.9 4.0 %fusion.95 = f32[4,1024,80]{1,2,0:T(8,128)S(1)} fusion(f32[4,512,1024]{2,1,0:T(8,128)S(1)} %get-tuple-element.301, f32[4,1024]{1,0:T(4,128)S(1)} %max.46, pred[1024,512]{0,1:T(8,128)(4,1)S(1)} %compare_and_fusion.5, f32[4,1024,80]{1,2,0:T(8,128)S(1)} %copy-done.3, f32[4,1024]{1,0:T(4,128)S(1)} %get-tuple-element.303, ...), kind=kOutput, calls=%fused_computation.21.clone.1 | convolution fusion | flops 346685440 | bytes 11894788 | tf_op jit(solution)/shard_map/while/body/krn,khn->krh/dot_general | solution.py:74
  173.2 4.6 %all-to-all-start.2 = ((f32[64,2,32]{2,1,0:T(2,128)}), f32[64,2,32]{2,1,0:T(2,128)S(1)}, u32[]{:S(2)}, u32[]{:S(2)}) async-start(f32[64,2,32]{2,1,0:T(2,128)} %copy.265), calls=%async_computation.2 | async-start | bytes 131072 | tf_op jit(solution)/shard_map/all_to_all | solution.py:175
  180.4 5.9 %all-to-all-done.2 = f32[64,2,32]{2,1,0:T(2,128)S(1)} async-done(((f32[64,2,32]{2,1,0:T(2,128)}), f32[64,2,32]{2,1,0:T(2,128)S(1)}, u32[]{:S(2)}, u32[]{:S(2)}) %all-to-all-start.2) | async-done | bytes 16416 | tf_op jit(solution)/shard_map/all_to_all | solution.py:175
  186.3 5.0 %all-to-all-start.4 = ((f32[64,2,32]{2,1,0:T(2,128)}), f32[64,2,32]{2,1,0:T(2,128)S(1)}, u32[]{:S(2)}, u32[]{:S(2)}) async-start(f32[64,2,32]{2,1,0:T(2,128)} %copy.279), calls=%async_computation.4 | async-start | bytes 131072 | tf_op jit(solution)/shard_map/all_to_all | solution.py:176
  193.9 1.4 gather_fusion.4
  195.4 1.8 copy.269
  197.2 1.9 copy.297
  199.1 4.8 %reshape.528 = f32[64,2,2560]{2,1,0:T(2,128)} reshape(f32[64,2,2,4,4,80]{5,4,3,2,1,0:T(4,128)} %copy.297) | data formatting | bytes 2621440 | tf_op jit(solution)/shard_map/reshape | solution.py:102
  203.9 10.2 %all-to-all-start.3 = ((f32[64,2,2560]{2,1,0:T(2,128)}), f32[64,2,2560]{2,1,0:T(2,128)}, u32[]{:S(2)}, u32[]{:S(2)}) async-start(f32[64,2,2560]{2,1,0:T(2,128)} %reshape.528), calls=%async_computation.3 | async-start | bytes 2621440 | tf_op jit(solution)/shard_map/all_to_all | solution.py:177
  214.4 6.5 %fusion.29 = f32[64,2,4,4,80]{4,3,1,2,0:T(4,128)} fusion(bf16[64,4,2,80,256]{4,3,2,1,0:T(8,128)(2,1)} %param.24, f32[64,4,2,4,256]{4,3,2,1,0:T(4,128)S(1)} %copy-done.8, f32[64,2,4,4]{3,1,2,0:T(2,128)S(1)} %copy-done.7, pred[64,256]{1,0:T(8,128)(4,1)S(1)} %copy-done.20), kind=kOutput, calls=%fused_computation.47 | convolution fusion | flops 86507520 | bytes 13533184 | tf_op jit(solution)/shard_map/stkjn,skhn->stkjh/dot_general | solution.py:216
  231.3 4.0 %reshape.398 = f32[128,2,4,4,80]{4,3,2,1,0:T(4,128)S(1)} reshape(f32[64,2,2560]{2,1,0:T(2,128)} %all-to-all-done.3) | data formatting | bytes 2621440 | tf_op jit(solution)/shard_map/reshape | solution.py:187
  235.4 2.1 gather_fusion.8
  237.5 2.1 gather_fusion.9
  239.5 5.0 %fusion.39 = bf16[64,2,4,4,80]{4,3,1,2,0:T(4,128)(2,1)S(1)} fusion(f32[64,2,4,4,80]{4,3,1,2,0:T(4,128)} %fusion.29, f32[64,2,4,4,80]{4,3,2,1,0:T(4,128)} %gather_fusion.9, f32[64,2,4,4,80]{4,3,2,1,0:T(4,128)} %gather_fusion.8, f32[64,2,4,4]{3,1,2,0:T(2,128)} %copy.282, f32[64,2,4,4]{3,1,2,0:T(2,128)} %copy.275, f32[64,2,4,4]{3,1,2,0:T(2,128)} %copy.273, ...), kind=kOutput, calls=%fused_computation.64 | convolution fusion | flops 2469888 | bytes 2433220 | tf_op jit(solution)/shard_map/stkju,sukh->stkjh/dot_general | solution.py:222
  245.3 5.0 %fusion.75 = f32[128,2560]{1,0:T(8,128)} fusion(bf16[128,1280]{1,0:T(8,128)(2,1)S(1)} %reshape.402, bf16[1280,2560]{1,0:T(8,128)(2,1)} %param.27), kind=kOutput, calls=%fused_computation.152 | convolution fusion | flops 838860800 | bytes 8192000 | tf_op jit(solution)/shard_map/dot_general | solution.py:239
  250.5 30.0 %all-reduce.2.cloned.1.call-done = f32[128,2560]{1,0:T(8,128)} async-done(((f32[128,2560]{1,0:T(8,128)}), f32[128,2560]{1,0:T(8,128)}) %all-reduce.2.cloned.1.call-update) | async-done | bytes 1310736 | tf_op jit(solution)/shard_map/psum | solution.py:242
  280.5 1.7 multiply_reduce_fusion
  (218 shorter events, 54.4 us)
Async XLA Ops:
  7.2 2.7 copy-start
  9.9 14.5 %copy-start.31 = (s32[64]{0:T(128)S(1)}, s32[64]{0:T(128)}, u32[]{:S(2)}) copy-start(s32[64]{0:T(128)} %param.20) | copy-start | bytes 772
  9.9 18.3 %copy-start.1 = (s32[48]{0:T(128)S(1)}, s32[48]{0:T(128)}, u32[]{:S(2)}) copy-start(s32[48]{0:T(128)} %param.19) | copy-start | bytes 580
  9.9 20.8 %copy-start.38 = (s32[64,1]{0,1:T(1,128)S(1)}, s32[64,1]{0,1:T(1,128)}, u32[]{:S(2)}) copy-start(s32[64,1]{0,1:T(1,128)} %param.21) | copy-start | bytes 772
  12.1 87.0 %all-to-all-start = ((s32[64,1,2]{2,1,0:T(1,128)}), s32[64,1,2]{2,1,0:T(1,128)}, u32[]{:S(2)}, u32[]{:S(2)}) async-start(s32[64,1,2]{2,1,0:T(1,128)} %copy.260), calls=%async_computation | async-start | bytes 65536 | tf_op jit(solution)/shard_map/all_to_all | solution.py:170
  31.5 13.6 %copy-start.2 = (bf16[64,2,2560]{2,1,0:T(2,128)(2,1)S(1)}, bf16[64,2,2560]{2,1,0:T(2,128)(2,1)}, u32[]{:S(2)}) copy-start(bf16[64,2,2560]{2,1,0:T(2,128)(2,1)} %param.18) | copy-start | bytes 1966084
  31.5 14.4 %copy-start.25 = (f32[2560]{0:T(1024)S(1)}, f32[2560]{0:T(1024)}, u32[]{:S(2)}) copy-start(f32[2560]{0:T(1024)} %param.25) | copy-start | bytes 30724
  58.3 2.9 copy-start.12
  58.3 2.9 copy-start.14
  64.8 3.1 %copy-start.6 = (f32[64,2,4,80]{3,0,2,1:T(8,128)S(1)}, f32[64,2,4,80]{3,0,2,1:T(8,128)}, u32[]{:S(2)}) copy-start(f32[64,2,4,80]{3,0,2,1:T(8,128)} %slice_bitcast_fusion.2) | copy-start | bytes 491524
  64.8 3.2 %copy-start.13 = (f32[64,2,80]{2,0,1:T(8,128)S(1)}, f32[64,2,80]{2,0,1:T(8,128)}, u32[]{:S(2)}) copy-start(f32[64,2,80]{2,0,1:T(8,128)} %copy-done.12) | copy-start | bytes 122884
  64.8 3.2 %copy-start.15 = (f32[64,2,80]{2,0,1:T(8,128)S(1)}, f32[64,2,80]{2,0,1:T(8,128)}, u32[]{:S(2)}) copy-start(f32[64,2,80]{2,0,1:T(8,128)} %copy-done.14) | copy-start | bytes 122884
  85.3 9.1 %copy-start.23 = (pred[64,2]{1,0:T(8,128)(4,1)S(1)}, pred[64,2]{1,0:T(8,128)(4,1)}, u32[]{:S(2)}) copy-start(pred[64,2]{1,0:T(8,128)(4,1)} %copy.252) | copy-start | bytes 388
  89.9 4.5 %copy-start.5 = (bf16[64,2,2560]{2,1,0:T(2,128)(2,1)S(1)}, bf16[64,2,2560]{2,1,0:T(2,128)(2,1)}, u32[]{:S(2)}) copy-start(bf16[64,2,2560]{2,1,0:T(2,128)(2,1)} %reshape.470) | copy-start | bytes 1966084
  89.9 4.5 %copy-start.24 = (pred[64,2]{1,0:T(8,128)(4,1)S(1)}, pred[64,2]{1,0:T(8,128)(4,1)}, u32[]{:S(2)}) copy-start(pred[64,2]{1,0:T(8,128)(4,1)} %copy.253) | copy-start | bytes 388
  99.1 22.8 %all-to-all-start.1 = ((bf16[64,2,2560]{2,1,0:T(2,128)(2,1)}), bf16[64,2,2560]{2,1,0:T(2,128)(2,1)}, u32[]{:S(2)}, u32[]{:S(2)}) async-start(bf16[64,2,2560]{2,1,0:T(2,128)(2,1)} %broadcast_select_fusion.1), calls=%async_computation.1 | async-start | bytes 1310720 | tf_op jit(solution)/shard_map/all_to_all | solution.py:169
  131.5 46.4 %copy-start.34 = (s32[64]{0:T(128)S(1)}, s32[64]{0:T(128)}, u32[]{:S(2)}) copy-start(s32[64]{0:T(128)} %gather_fusion.5) | copy-start | bytes 772
  131.5 46.4 %copy-start.35 = (s32[64]{0:T(128)S(1)}, s32[64]{0:T(128)}, u32[]{:S(2)}) copy-start(s32[64]{0:T(128)} %gather_fusion.3) | copy-start | bytes 772
  131.5 46.4 %copy-start.40 = (s32[64]{0:T(128)S(1)}, s32[64]{0:T(128)}, u32[]{:S(2)}) copy-start(s32[64]{0:T(128)} %copy-done.39) | copy-start | bytes 772
  134.2 2.2 copy-start.3
  140.3 1.1 copy-start.4
  144.0 2.2 copy-start.3
  150.2 1.1 copy-start.4
  153.9 2.2 copy-start.3
  160.0 1.1 copy-start.4
  163.7 2.2 copy-start.3
  169.9 1.1 copy-start.4
  171.3 20.0 %copy-start.7 = (f32[64,2,4,4]{3,1,2,0:T(2,128)S(1)}, f32[64,2,4,4]{3,1,2,0:T(2,128)}, u32[]{:S(2)}) copy-start(f32[64,2,4,4]{3,1,2,0:T(2,128)} %copy.247) | copy-start | bytes 24580
  171.3 20.0 %copy-start.16 = (f32[64,2,4,4,2]{3,4,1,2,0:T(2,128)S(1)}, f32[64,2,4,4,2]{3,4,1,2,0:T(2,128)}, u32[]{:S(2)}) copy-start(f32[64,2,4,4,2]{3,4,1,2,0:T(2,128)} %get-tuple-element.225) | copy-start | bytes 49156
  171.3 20.0 %copy-start.37 = (pred[2,2]{1,0:T(4,128)(4,1)S(1)}, pred[2,2]{1,0:T(4,128)(4,1)}, u32[]{:S(2)}) copy-start(pred[2,2]{1,0:T(4,128)(4,1)} %iota_compare_fusion.4) | copy-start | bytes 16
  171.4 21.8 %copy-start.11 = (f32[64,2,4,4]{3,1,2,0:T(2,128)S(1)}, f32[64,2,4,4]{3,1,2,0:T(2,128)}, u32[]{:S(2)}) copy-start(f32[64,2,4,4]{3,1,2,0:T(2,128)} %fusion.46) | copy-start | bytes 24580
  173.2 13.1 %all-to-all-start.2 = ((f32[64,2,32]{2,1,0:T(2,128)}), f32[64,2,32]{2,1,0:T(2,128)S(1)}, u32[]{:S(2)}, u32[]{:S(2)}) async-start(f32[64,2,32]{2,1,0:T(2,128)} %copy.265), calls=%async_computation.2 | async-start | bytes 131072 | tf_op jit(solution)/shard_map/all_to_all | solution.py:175
  186.3 9.1 %copy-start.17 = (f32[64,2,32]{2,1,0:T(2,128)}, f32[64,2,32]{2,1,0:T(2,128)S(1)}, u32[]{:S(2)}) copy-start(f32[64,2,32]{2,1,0:T(2,128)S(1)} %all-to-all-done.2) | copy-start | bytes 49156
  186.3 17.6 %all-to-all-start.4 = ((f32[64,2,32]{2,1,0:T(2,128)}), f32[64,2,32]{2,1,0:T(2,128)S(1)}, u32[]{:S(2)}, u32[]{:S(2)}) async-start(f32[64,2,32]{2,1,0:T(2,128)} %copy.279), calls=%async_computation.4 | async-start | bytes 131072 | tf_op jit(solution)/shard_map/all_to_all | solution.py:176
  203.9 10.4 %copy-start.29 = (s32[64]{0:T(128)S(1)}, s32[64]{0:T(128)}, u32[]{:S(2)}) copy-start(s32[64]{0:T(128)} %get-tuple-element.207) | copy-start | bytes 772
  203.9 10.4 %copy-start.30 = (s32[64]{0:T(128)S(1)}, s32[64]{0:T(128)}, u32[]{:S(2)}) copy-start(s32[64]{0:T(128)} %get-tuple-element.221) | copy-start | bytes 772
  203.9 10.5 %copy-start.8 = (f32[64,4,2,4,256]{4,3,2,1,0:T(4,128)S(1)}, f32[64,4,2,4,256]{4,3,2,1,0:T(4,128)}, u32[]{:S(2)}) copy-start(f32[64,4,2,4,256]{4,3,2,1,0:T(4,128)} %get-tuple-element.223) | copy-start | bytes 6291460
  203.9 10.5 %copy-start.20 = (pred[64,256]{1,0:T(8,128)(4,1)S(1)}, pred[64,256]{1,0:T(8,128)(4,1)}, u32[]{:S(2)}) copy-start(pred[64,256]{1,0:T(8,128)(4,1)} %iota_compare_fusion) | copy-start | bytes 49156
  203.9 10.4 %copy-start.18 = (f32[64,2,32]{2,1,0:T(2,128)}, f32[64,2,32]{2,1,0:T(2,128)S(1)}, u32[]{:S(2)}) copy-start(f32[64,2,32]{2,1,0:T(2,128)S(1)} %all-to-all-done.4) | copy-start | bytes 49156
  203.9 27.4 %all-to-all-start.3 = ((f32[64,2,2560]{2,1,0:T(2,128)}), f32[64,2,2560]{2,1,0:T(2,128)}, u32[]{:S(2)}, u32[]{:S(2)}) async-start(f32[64,2,2560]{2,1,0:T(2,128)} %reshape.528), calls=%async_computation.3 | async-start | bytes 2621440 | tf_op jit(solution)/shard_map/all_to_all | solution.py:177
  214.1 66.4 %all-reduce.2.cloned.1.call-start = ((), (), s32[]{:S(2)}) async-start(), calls=%async_computation.5 | async-start | bytes 2621440 | tf_op jit(solution)/shard_map/psum | solution.py:242
  220.9 6.0 %copy-start.19 = (f32[64,2,4,4]{0,3,2,1:T(4,128)S(1)}, f32[64,2,4,4]{0,3,2,1:T(4,128)}, u32[]{:S(2)}) copy-start(f32[64,2,4,4]{0,3,2,1:T(4,128)} %max.20) | copy-start | bytes 24580
  220.9 6.0 %copy-start.21 = (f32[64,2,4,4]{0,3,2,1:T(4,128)S(1)}, f32[64,2,4,4]{0,3,2,1:T(4,128)}, u32[]{:S(2)}) copy-start(f32[64,2,4,4]{0,3,2,1:T(4,128)} %copy.277) | copy-start | bytes 24580
  220.9 6.0 %copy-start.22 = (f32[64,2,4,4]{0,3,2,1:T(4,128)S(1)}, f32[64,2,4,4]{0,3,2,1:T(4,128)}, u32[]{:S(2)}) copy-start(f32[64,2,4,4]{0,3,2,1:T(4,128)} %copy.276) | copy-start | bytes 24580
  220.9 6.1 %copy-start.32 = (pred[64]{0:T(512)(128)(4,1)S(1)}, pred[64]{0:T(512)(128)(4,1)}, u32[]{:S(2)}) copy-start(pred[64]{0:T(512)(128)(4,1)} %gather_fusion.4) | copy-start | bytes 196
  237.5 2.1 copy-start.33
  250.2 30.3 %copy-start.26 = (f32[2560]{0:T(1024)S(1)}, f32[2560]{0:T(1024)}, u32[]{:S(2)}) copy-start(f32[2560]{0:T(1024)} %param.29) | copy-start | bytes 30724
  250.2 30.3 %copy-start.27 = (f32[2560]{0:T(1024)S(1)}, f32[2560]{0:T(1024)}, u32[]{:S(2)}) copy-start(f32[2560]{0:T(1024)} %param.28) | copy-start | bytes 30724
  (5 other events, 4.2 us)
Sparse Core Ops, SparseCore 0:
  250.4 30.0 all-reduce.1
where the time goes:
time: 297 us; the launch traced here: 291 us
  local copies, waits for them, and re-layouts  89.2 us (30%)
  matrix products  61.2 us (21%)
  waiting for transfers between devices  47.4 us (16%)
  starting transfers between devices  42.1 us (14%)
  other arithmetic  31.9 us (11%)
  between operations  18.8 us (6%)
    psum x1, waiting for transfers between devices, local(): head_total = lax.psum(mixed, 'tp')  30 us
    unnamed x81, local copies, waits for them, and re-layouts  17.9 us
    dot_general x4, matrix products, key_step(): jnp.einsum('krn,khn->krh', weights.astype(jnp.bfloat16), value_part, pref...  15.8 us
    all_to_all x1, starting transfers between devices, local(): lax.all_to_all(send_tails, 'grp', split_axis=0, concat_axis=0, tiled=True)  12.2 us
    all_to_all x1, waiting for transfers between devices, local(): lax.all_to_all(send_queries, 'grp', split_axis=0, concat_axis=0, tiled=True)  10.5 us
    all_to_all x1, starting transfers between devices, local(): lax.all_to_all(part_acc, 'grp', split_axis=0, concat_axis=0, tiled=True)  10.2 us
    all_to_all x1, starting transfers between devices, local(): lax.all_to_all(send_queries, 'grp', split_axis=0, concat_axis=0, tiled=True)  9.93 us
    reduce_sum x4, other arithmetic, key_step(): run_sum = run_sum * factor + jnp.sum(weights, axis=-1)  8.47 us
  transfers between devices with their start and end apart: 6, of which 4 were waited for; matrix products, arithmetic and copies ran while one was open for 35% of the time, Pallas kernels for 0%

commit v1 on v0

v1 whole, which is shorter than its diff:
```python
import functools

import jax
import jax.numpy as jnp
import numpy as np
from jax import lax
from jax.experimental import pallas as pl
from jax.experimental.pallas import tpu as pltpu
from jax.sharding import PartitionSpec as P

W = 4096
HD = 80
EPS = 1e-05
ROPE_BASE = 10000.0
NEG = -1e30
MESH = pl.DeviceIdType.MESH
F32 = jnp.float32
BF16 = jnp.bfloat16
LOG2E = 1.4426950408889634
SCALE2 = HD**-0.5 * LOG2E
WIDE = 384
SIDE = 320


def iota(shape, dim):
    return lax.broadcasted_iota(jnp.int32, shape, dim)


def to_row(col, size):
    eye = iota((size, size), 0) == iota((size, size), 1)
    return jnp.sum(jnp.where(eye, col, 0.0), axis=0, keepdims=True)


def to_col(row, size):
    eye = iota((size, size), 0) == iota((size, size), 1)
    return jnp.sum(jnp.where(eye, row, 0.0), axis=1, keepdims=True)


def split3(x):
    hi = x.astype(BF16).astype(F32)
    rest = x - hi
    mid = rest.astype(BF16).astype(F32)
    low = (rest - mid).astype(BF16).astype(F32)
    return hi, mid, low


def sample_codes(req, rank_scale, samples):
    req_row = to_row(req, samples)
    shape = (samples, samples)
    before = (req == req_row) & (iota(shape, 1) < iota(shape, 0))
    rank = jnp.sum(jnp.where(before, 1.0, 0.0), axis=1, keepdims=True)
    return req * rank_scale + rank


def qkv_kernel(
    x_ref, req_ref, tail_ref, plen_ref, slot_ref, gain_ref, freq_ref, w_ref,
    send_ref, qt_ref, qb_ref, own_ref, normed, acc,
):
    step = pl.program_id(0)
    last = pl.num_programs(0) - 1
    n = x_ref.shape[0]
    d = x_ref.shape[1] // 2
    chunks, _, width = normed.shape

    @pl.when(step == 0)
    def _():
        for t in range(2):
            x = x_ref[:, t * d : (t + 1) * d].astype(F32)
            r = lax.rsqrt(jnp.mean(x * x, axis=-1, keepdims=True) + EPS)
            y = (x * r * gain_ref[...]).astype(BF16)
            for c in range(chunks):
                normed[c, t * n : (t + 1) * n, :] = y[:, c * width : (c + 1) * width]

    part = jnp.dot(normed[step], w_ref[...], preferred_element_type=F32)

    @pl.when(step == 0)
    def _():
        acc[...] = part

    @pl.when(step > 0)
    def _():
        acc[...] += part

    @pl.when(step == last)
    def _():
        req = req_ref[...].astype(F32)
        plen = plen_ref[...].astype(F32)
        reqs = plen.shape[1]
        slots = slot_ref.shape[1]
        owned = req == iota((n, reqs), 1).astype(F32)
        length = jnp.sum(jnp.where(owned, plen, 0.0), axis=1, keepdims=True)
        tail = to_col(tail_ref[...].astype(F32), n)
        pos = length + tail
        pos = jnp.concatenate([pos, pos + 1.0], axis=0)
        angle = pos * freq_ref[...]
        cosine = jnp.cos(angle)
        sine = jnp.sin(angle)
        half = HD // 2
        sine = jnp.where(iota(sine.shape, 1) < half, -sine, sine)

        def rope(u):
            turned = jnp.concatenate([u[:, half:], u[:, :half]], axis=1)
            return u * cosine + turned * sine

        own_ref[...] = jnp.zeros_like(own_ref)
        for k in range(4):
            base = k * 6 * HD
            for j in range(4):
                u = rope(acc[:, base + j * HD : base + (j + 1) * HD]).astype(BF16)
                for t in range(2):
                    row = (t * 4 + j) * n
                    qb_ref[row : row + n, k * HD : (k + 1) * HD] = u[t * n : (t + 1) * n]
            key = rope(acc[:, base + 4 * HD : base + 5 * HD]).astype(BF16).astype(F32)
            value = acc[:, base + 5 * HD : base + 6 * HD].astype(BF16).astype(F32)
            for t in range(2):
                own_ref[t, :, k * HD : (k + 1) * HD] = key[t * n : (t + 1) * n]
                own_ref[2 + t, :, k * HD : (k + 1) * HD] = value[t * n : (t + 1) * n]
        side = jnp.broadcast_to(tail, (n, WIDE - SIDE)).astype(BF16)
        for tj in range(8):
            qb_ref[tj * n : (tj + 1) * n, SIDE:] = side

        code = sample_codes(req, 2.0, n)
        cols = 8 * n
        rows = slots * 16
        spread = iota((n, cols), 0) == (iota((n, cols), 1) & (n - 1))
        code_row = jnp.sum(jnp.where(spread, code, 0.0), axis=0, keepdims=True)
        spread = iota((rows, slots), 1) == (iota((rows, slots), 0) >> 4)
        slot = slot_ref[...].astype(F32)
        slot_col = jnp.sum(jnp.where(spread, slot, 0.0), axis=1, keepdims=True)
        item = ((iota((rows, 1), 0) >> 3) & 1).astype(F32)
        want = slot_col * 2.0 + item
        pick = (want == code_row) & (
            (iota((rows, cols), 0) & 7) == (iota((rows, cols), 1) // n)
        )
        pick = jnp.where(pick, 1.0, 0.0).astype(BF16)
        packed = qb_ref[...]
        send_ref[...] = jnp.dot(pick, packed, preferred_element_type=F32).astype(BF16)
        r = iota((cols, cols), 0)
        c = iota((cols, cols), 1)
        perm = ((r >> 3) == (c & (n - 1))) & ((r & 7) == (c // n))
        perm = jnp.where(perm, 1.0, 0.0).astype(BF16)
        qt_ref[...] = jnp.dot(perm, packed, preferred_element_type=F32)


def qkv(x, req, tail, plen, slot, gain, freq, w):
    n = x.shape[0]
    d = x.shape[1] // 2
    chunks = 5
    width = d // chunks
    slots = slot.shape[1]
    full = lambda a: pl.BlockSpec(a.shape, lambda i: (0,) * a.ndim)
    whole = lambda *s: pl.BlockSpec(s, lambda i: (0,) * len(s))
    return pl.pallas_call(
        qkv_kernel,
        grid=(chunks,),
        in_specs=[full(a) for a in (x, req, tail, plen, slot, gain, freq)]
        + [pl.BlockSpec((width, w.shape[1]), lambda i: (i, 0))],
        out_specs=[
            whole(slots * 16, WIDE), whole(8 * n, WIDE), whole(8 * n, WIDE), whole(4, n, WIDE),
        ],
        out_shape=[
            jax.ShapeDtypeStruct((slots * 16, WIDE), BF16),
            jax.ShapeDtypeStruct((8 * n, WIDE), F32),
            jax.ShapeDtypeStruct((8 * n, WIDE), BF16),
            jax.ShapeDtypeStruct((4, n, WIDE), F32),
        ],
        scratch_shapes=[
            pltpu.VMEM((chunks, 2 * n, width), BF16),
            pltpu.VMEM((2 * n, w.shape[1]), F32),
        ],
        compiler_params=pltpu.CompilerParams(vmem_limit_bytes=60 << 20),
        name="qkv",
    )(x, req, tail, plen, slot, gain, freq, w)


def exchange_kernel(groups, rows, s_ref, r_ref, send_sem, recv_sem, own_sem):
    me = lax.axis_index("grp")
    barrier = pltpu.get_barrier_semaphore()

    def greet(d, _):
        peer = lax.rem(me + d, groups)
        pl.semaphore_signal(barrier, inc=1, device_id={"grp": peer}, device_id_type=MESH)
        return 0

    lax.fori_loop(1, groups, greet, 0)

    def block(ref, i):
        return ref.at[pl.ds(pl.multiple_of(i * rows, rows), rows)]

    own = pltpu.make_async_copy(block(s_ref, me), block(r_ref, me), own_sem)
    own.start()
    pl.semaphore_wait(barrier, groups - 1)

    def copy_to(d):
        peer = lax.rem(me + d, groups)
        return pltpu.make_async_remote_copy(
            src_ref=block(s_ref, peer),
            dst_ref=block(r_ref, me),
            send_sem=send_sem.at[d],
            recv_sem=recv_sem.at[d],
            device_id={"grp": peer},
            device_id_type=MESH,
        )

    def send(d, _):
        copy_to(d).start()
        return 0

    def finish(d, _):
        copy_to(d).wait()
        return 0

    lax.fori_loop(1, groups, send, 0)
    lax.fori_loop(1, groups, finish, 0)
    own.wait()


def exchange(s, groups, number):
    rows = s.shape[0] // groups
    return pl.pallas_call(
        functools.partial(exchange_kernel, groups, rows),
        out_shape=jax.ShapeDtypeStruct(s.shape, s.dtype),
        in_specs=[pl.BlockSpec(memory_space=pl.ANY)],
        out_specs=pl.BlockSpec(memory_space=pl.ANY),
        scratch_shapes=[
            pltpu.SemaphoreType.DMA((groups,)),
            pltpu.SemaphoreType.DMA((groups,)),
            pltpu.SemaphoreType.DMA,
        ],
        compiler_params=pltpu.CompilerParams(collective_id=number, has_side_effects=True),
        name="exchange" + str(number),
    )(s)


def store_side(ref, rows, logs):
    n = logs[0].shape[0]
    lane = iota((n, WIDE - SIDE), 1)
    side = jnp.where(lane == 12, 1.0, 0.0)
    for k, value in enumerate(logs):
        for p, term in enumerate(split3(value)):
            side = jnp.where(lane == 4 * p + k, term, side)
    ref[rows, SIDE:] = side.astype(ref.dtype)


def tail_kernel(q_ref, kv_ref, o_ref):
    n = kv_ref.shape[0]
    length = kv_ref.shape[4]
    scores = []
    limits = []
    for s in range(n):
        limit = q_ref[s * 8 : (s + 1) * 8, SIDE : SIDE + 1]
        for k in range(4):
            q = q_ref[s * 8 : (s + 1) * 8, k * HD : (k + 1) * HD].astype(BF16)
            scores.append(jnp.dot(q, kv_ref[s, k, 0], preferred_element_type=F32))
            limits.append(limit)
    score = jnp.concatenate(scores, axis=0) * SCALE2
    limit = jnp.concatenate(limits, axis=0)
    at = iota(score.shape, 1).astype(F32)
    score = jnp.where(at < limit, score, NEG)
    top = jnp.max(score, axis=1, keepdims=True)
    weight = jnp.exp2(score - top)
    total = jnp.sum(weight, axis=1, keepdims=True)
    inverse = 1.0 / total
    logs = top + jnp.log2(total)
    weight = weight.astype(BF16)
    for s in range(n):
        rows = slice(s * 8, (s + 1) * 8)
        parts = []
        for k in range(4):
            at = slice((s * 4 + k) * 8, (s * 4 + k + 1) * 8)
            out = lax.dot_general(
                weight[at], kv_ref[s, k, 1], (((1,), (1,)), ((), ())),
                preferred_element_type=F32,
            )
            o_ref[rows, k * HD : (k + 1) * HD] = out * inverse[at]
            parts.append(logs[at])
        store_side(o_ref, rows, parts)


def tail_attention(qt, kv):
    n = kv.shape[0]
    step = 8
    return pl.pallas_call(
        tail_kernel,
        grid=(n // step,),
        in_specs=[
            pl.BlockSpec((step * 8, WIDE), lambda i: (i, 0)),
            pl.BlockSpec((step,) + kv.shape[1:], lambda i: (i, 0, 0, 0, 0)),
        ],
        out_specs=pl.BlockSpec((step * 8, WIDE), lambda i: (i, 0)),
        out_shape=jax.ShapeDtypeStruct((n * 8, WIDE), F32),
        compiler_params=pltpu.CompilerParams(vmem_limit_bytes=60 << 20),
        name="tail",
    )(qt, kv)


def slot_kernel(q_ref, kv_ref, slot_ref, plen_ref, o_ref):
    rows = q_ref.shape[0]
    length = kv_ref.shape[4]
    slots = slot_ref.shape[1]
    reqs = plen_ref.shape[1]
    me = lax.axis_index("grp")
    slot = slot_ref[...].astype(F32)
    at = iota((1, slots), 1)
    mine = jnp.sum(jnp.where(at == me, slot, 0.0), axis=1, keepdims=True)
    part = jnp.sum(jnp.where((slot == mine) & (at < me), 1.0, 0.0), axis=1, keepdims=True)
    owned = iota((1, reqs), 1).astype(F32) == mine
    tokens = jnp.sum(jnp.where(owned, plen_ref[...].astype(F32), 0.0), axis=1, keepdims=True)
    cached = jnp.minimum(tokens, float(W))
    start = part * float(length)
    index = iota((1, length), 1).astype(F32)
    bias = jnp.where(index < cached - start, 0.0, NEG)
    sub = 128
    near = 384
    for b in range(rows // sub):
        span = slice(b * sub, (b + 1) * sub)
        tail = q_ref[span, SIDE : SIDE + 128 - SIDE % 128].astype(F32)[:, 0:1]
        token = ((iota((sub, 1), 0) >> 2) & 1).astype(F32)
        floor = tail + token + (cached - float(W)) - start
        logs = []
        for k in range(4):
            q = q_ref[span, k * HD : (k + 1) * HD]
            score = jnp.dot(q, kv_ref[0, k, 0], preferred_element_type=F32)
            score = score * SCALE2 + bias
            head = jnp.where(index[:, :near] > floor, score[:, :near], NEG)
            score = jnp.concatenate([head, score[:, near:]], axis=1)
            top = jnp.max(score, axis=1, keepdims=True)
            weight = jnp.exp2(score - top)
            total = jnp.sum(weight, axis=1, keepdims=True)
            out = lax.dot_general(
                weight.astype(BF16), kv_ref[0, k, 1], (((1,), (1,)), ((), ())),
                preferred_element_type=F32,
            )
            o_ref[span, k * HD : (k + 1) * HD] = (out * (1.0 / total)).astype(BF16)
            logs.append(top + jnp.log2(total))
        store_side(o_ref, span, logs)


def slot_attention(r, kv, slot, plen):
    rows = r.shape[0]
    step = min(rows, 256)
    full = lambda a: pl.BlockSpec(a.shape, lambda i: (0,) * a.ndim)
    return pl.pallas_call(
        slot_kernel,
        grid=(rows // step,),
        in_specs=[pl.BlockSpec((step, WIDE), lambda i: (i, 0)), full(kv), full(slot), full(plen)],
        out_specs=pl.BlockSpec((step, WIDE), lambda i: (i, 0)),
        out_shape=jax.ShapeDtypeStruct((rows, WIDE), BF16),
        compiler_params=pltpu.CompilerParams(vmem_limit_bytes=60 << 20),
        name="slot",
    )(r, kv, slot, plen)


def mix_kernel(b_ref, t_ref, qb_ref, own_ref, req_ref, slot_ref, wo_ref, m_ref, mb_ref, att):
    @pl.when(pl.program_id(0) == 0)
    def _():
        n = own_ref.shape[1]
        slots = slot_ref.shape[1]
        rows = 8 * n
        back = slots * 16
        code = sample_codes(req_ref[...].astype(F32), 4.0, n)
        spread = iota((rows, n), 1) == (iota((rows, n), 0) & (n - 1))
        code = jnp.sum(jnp.where(spread, to_row(code, n), 0.0), axis=1, keepdims=True)
        slot = slot_ref[...].astype(F32)
        slot_col = to_col(slot, slots)
        earlier = (slot == slot_col) & (iota((slots, slots), 1) < iota((slots, slots), 0))
        part = jnp.sum(jnp.where(earlier, 1.0, 0.0), axis=1, keepdims=True)
        key = slot_col * 4.0 + part * 2.0
        spread = iota((slots, back), 0) == (iota((slots, back), 1) >> 4)
        key = jnp.sum(jnp.where(spread, key, 0.0), axis=0, keepdims=True)
        key = key + ((iota((1, back), 1) >> 3) & 1).astype(F32)
        same = (iota((rows, back), 0) // n) == (iota((rows, back), 1) & 7)
        code = jnp.where(same, code, -8.0)
        returned = b_ref[...]
        parts = []
        for p in range(2):
            pick = jnp.where(key == code + 2.0 * p, 1.0, 0.0).astype(BF16)
            parts.append(jnp.dot(pick, returned, preferred_element_type=F32))
        r = iota((rows, rows), 0)
        c = iota((rows, rows), 1)
        perm = ((c >> 3) == (r & (n - 1))) & ((c & 7) == (r // n))
        perm = jnp.where(perm, 1.0, 0.0).astype(BF16)
        parts.append(jnp.dot(perm, t_ref[...].astype(BF16), preferred_element_type=F32))

        l = iota((WIDE, 128), 0)
        c = iota((WIDE, 128), 1)
        gather = (l >= SIDE) & (l < SIDE + 12) & (((l - SIDE) & 3) == c)
        gather = jnp.where(gather, 1.0, 0.0).astype(BF16)
        segment = jnp.where((l // HD == c) & (c < 4), 1.0, 0.0)
        logs = [jnp.dot(x.astype(BF16), gather, preferred_element_type=F32) for x in parts]
        logs[1] = jnp.where(parts[1][:, SIDE + 12 : SIDE + 13] > 0.5, logs[1], NEG)
        query = qb_ref[...].astype(F32)
        values = [x for x in parts]
        for u in range(2):
            keys = jnp.concatenate([own_ref[u]] * 8, axis=0)
            s = jnp.dot(
                query * keys, segment, preferred_element_type=F32,
                precision=lax.Precision.HIGHEST,
            ) * SCALE2
            if u:
                s = jnp.where(iota(s.shape, 0) >= 4 * n, s, NEG)
            logs.append(s)
            values.append(jnp.concatenate([own_ref[2 + u]] * 8, axis=0))
        top = functools.reduce(jnp.maximum, logs)
        weights = [jnp.exp2(x - top) for x in logs]
        inverse = 1.0 / functools.reduce(jnp.add, weights)
        lane = iota((rows, WIDE), 1)
        out = jnp.zeros((rows, WIDE), F32)
        for w, v in zip(weights, values):
            w = w * inverse
            wide = jnp.broadcast_to(w[:, 3:4], (rows, WIDE))
            for k in (2, 1, 0):
                wide = jnp.where(lane < (k + 1) * HD, w[:, k : k + 1], wide)
            out += wide * v
        out = out.astype(BF16)
        for k in range(4):
            for j in range(4):
                for t in range(2):
                    row = (t * 4 + j) * n
                    att[t * n : (t + 1) * n, (k * 4 + j) * HD : (k * 4 + j + 1) * HD] = out[
                        row : row + n, k * HD : (k + 1) * HD
                    ]

    mixed = jnp.dot(att[...], wo_ref[...], preferred_element_type=F32)
    m_ref[...] = mixed
    mb_ref[...] = mixed.astype(BF16)


def mix(b, t, qb, own, req, slot, wo):
    n = own.shape[1]
    d = wo.shape[1]
    width = 512
    full = lambda a: pl.BlockSpec(a.shape, lambda i: (0,) * a.ndim)
    return pl.pallas_call(
        mix_kernel,
        grid=(d // width,),
        in_specs=[full(a) for a in (b, t, qb, own, req, slot)]
        + [pl.BlockSpec((wo.shape[0], width), lambda i: (0, i))],
        out_specs=[pl.BlockSpec((2 * n, width), lambda i: (0, i))] * 2,
        out_shape=[
            jax.ShapeDtypeStruct((2 * n, d), F32),
            jax.ShapeDtypeStruct((2 * n, d), BF16),
        ],
        scratch_shapes=[pltpu.VMEM((2 * n, wo.shape[0]), BF16)],
        compiler_params=pltpu.CompilerParams(vmem_limit_bytes=60 << 20),
        name="mix",
    )(b, t, qb, own, req, slot, wo)


def finish_kernel(m_ref, mb_ref, x_ref, gain_ref, w_ref, h_ref, s_ref, got, send_sem, recv_sem):
    tp = lax.axis_index("tp")
    partner = {"tp": 1 - tp}
    barrier = pltpu.get_barrier_semaphore()
    pl.semaphore_signal(barrier, inc=1, device_id=partner, device_id_type=MESH)
    pl.semaphore_wait(barrier, 1)
    copy = pltpu.make_async_remote_copy(
        src_ref=mb_ref, dst_ref=got, send_sem=send_sem, recv_sem=recv_sem,
        device_id=partner, device_id_type=MESH,
    )
    copy.start()
    n = x_ref.shape[0]
    d = x_ref.shape[1] // 2
    share = d // 2
    scale = gain_ref[...] * w_ref[...]
    copy.wait()
    mine = pl.multiple_of(tp * share, 128)
    for t in range(2):
        rows = slice(t * n, (t + 1) * n)
        total = (
            x_ref[:, t * d : (t + 1) * d].astype(F32) + m_ref[rows, :] + got[rows, :].astype(F32)
        )
        square = jnp.mean(total * total, axis=-1, keepdims=True)
        score = jnp.sum(total * scale, axis=-1, keepdims=True) * lax.rsqrt(square + EPS)
        s_ref[:, t : t + 1] = score
        at = pl.multiple_of(tp * share + t * d, 128)
        h_ref[:, t * share : (t + 1) * share] = (
            x_ref[:, pl.ds(at, share)].astype(F32)
            + m_ref[rows, pl.ds(mine, share)]
            + got[rows, pl.ds(mine, share)].astype(F32)
        )


def finish(m, mb, x, gain, w):
    n = x.shape[0]
    d = x.shape[1] // 2
    vmem = pl.BlockSpec(memory_space=pltpu.VMEM)
    return pl.pallas_call(
        finish_kernel,
        in_specs=[vmem] * 5,
        out_specs=[vmem] * 2,
        out_shape=[
            jax.ShapeDtypeStruct((n, d), F32),
            jax.ShapeDtypeStruct((n, 2), F32),
        ],
        scratch_shapes=[
            pltpu.VMEM((2 * n, d), BF16),
            pltpu.SemaphoreType.DMA,
            pltpu.SemaphoreType.DMA,
        ],
        compiler_params=pltpu.CompilerParams(collective_id=7, has_side_effects=True),
        name="finish",
    )(m, mb, x, gain, w)


def local(
    hidden_in, prompt_len, slot_req, sample_req, tail_len, slot_kv, tail_kv,
    attn_gain, wqkv, wo, out_gain, score_w,
):
    n, _, d = hidden_in.shape
    groups = lax.axis_size("grp")
    x = hidden_in.reshape(n, 2 * d)
    tail = tail_len.reshape(1, n)
    plen = prompt_len.reshape(1, -1)
    slot = slot_req.reshape(1, -1)
    half = HD // 2
    freq = ROPE_BASE ** (-np.arange(half, dtype=np.float64) / half)
    freq = jnp.asarray(np.concatenate([freq, freq])[None, :], F32)
    send, qt, qb, own = qkv(x, sample_req, tail, plen, slot, attn_gain.reshape(1, d), freq, wqkv)
    got = exchange(send, groups, 0)
    tails = tail_attention(qt, tail_kv)
    part = slot_attention(got, slot_kv, slot, plen)
    back = exchange(part, groups, 1)
    m, mb = mix(back, tails, qb, own, sample_req, slot, wo)
    h, score = finish(m, mb, x, out_gain.reshape(1, d), score_w.reshape(1, d))
    return (h.reshape(n, 2, d // 2), score)


def solution(mesh):
    in_specs = (
        P("grp", None, None),
        P(),
        P(),
        P("grp", None),
        P("grp"),
        P("grp", "tp", None, None, None),
        P("grp", "tp", None, None, None),
        P(),
        P(None, "tp"),
        P("tp", None),
        P(),
        P(),
    )
    out_specs = (P("grp", None, "tp"), P("grp", None))
    return jax.shard_map(local, mesh=mesh, in_specs=in_specs, out_specs=out_specs, check_vma=False)
```

time: 297 us -> 112 us (0.38); the launches traced: 291 us -> 111 us
  Pallas kernels: 0 us -> 101 us
  local copies, waits for them, and re-layouts: 89.2 us -> 9.62 us
  matrix products: 61.2 us -> 0 us
  waiting for transfers between devices: 47.4 us -> 0 us
  starting transfers between devices: 42.1 us -> 0 us
  other arithmetic: 31.9 us -> 0 us
  between operations: 18.8 us -> 0.66 us
    pallas_call x0 -> x7, Pallas kernels: none -> 101 us  [the longest x2 38.3 us: exchange(): pl.pallas_call(functools.partial(exchange_kernel, groups, rows), out_shap...]
    dot_general x14 -> x0, matrix products: 61.2 us -> none  [the longest x4 15.8 us: key_step(): jnp.einsum('krn,khn->krh', weights.astype(jnp.bfloat16), value_part, pref...]
    all_to_all x5 -> x0, starting transfers between devices: 41.9 us -> none  [the longest x1 12.2 us: local(): lax.all_to_all(send_tails, 'grp', split_axis=0, concat_axis=0, tiled=True)]
    psum x1 -> x0, waiting for transfers between devices: 30 us -> none  [local(): head_total = lax.psum(mixed, 'tp')]
    reduce_sum x11 -> x0, other arithmetic: 18.8 us -> none  [the longest x4 8.47 us: key_step(): run_sum = run_sum * factor + jnp.sum(weights, axis=-1)]
    reshape x13 -> x4, local copies, waits for them, and re-layouts: 22.5 us -> 4.87 us  [the longest x1 2.36 us: local(): return (h.reshape(n, 2, d // 2), score)]
    all_to_all x5 -> x0, waiting for transfers between devices: 17.3 us -> none  [the longest x1 10.5 us: local(): lax.all_to_all(send_queries, 'grp', split_axis=0, concat_axis=0, tiled=True)]
    gather x19 -> x0, local copies, waits for them, and re-layouts: 16.2 us -> none  [the longest x1 2.09 us: local(): acc_one = jnp.take(flat_acc, index_one, axis=0)]
  transfers between devices with their start and end apart: 6 -> 0, of which waited for: 4 -> 0; matrix products, arithmetic and copies ran while one was open for 35% -> 0% of each run, Pallas kernels for 0% -> 0%
where the time goes in v1:
time: 112 us; the launch traced here: 111 us
  Pallas kernels  101 us (90%)
  local copies, waits for them, and re-layouts  9.62 us (9%)
    pallas_call x2, Pallas kernels, exchange(): pl.pallas_call(functools.partial(exchange_kernel, groups, rows), out_shap...  38.3 us
    pallas_call x1, Pallas kernels, slot_attention(): pl.pallas_call(slot_kernel, grid=(rows // step,), in_specs=[pl.BlockSpec(...  17.5 us
    pallas_call x1, Pallas kernels, tail_attention(): pl.pallas_call(tail_kernel, grid=(n // step,), in_specs=[pl.BlockSpec((st...  13.4 us
    pallas_call x1, Pallas kernels, mix(): pl.pallas_call(mix_kernel, grid=(d // width,), in_specs=[full(a) for a in...  12.3 us
    pallas_call x1, Pallas kernels, qkv(): pl.pallas_call(qkv_kernel, grid=(chunks,), in_specs=[full(a) for a in (x,...  12.2 us
    pallas_call x1, Pallas kernels, finish(): pl.pallas_call(finish_kernel, in_specs=[vmem] * 5, out_specs=[vmem] * 2,...  7.51 us
    unnamed x7, local copies, waits for them, and re-layouts  4.75 us
    reshape x1, local copies, waits for them, and re-layouts, local(): return (h.reshape(n, 2, d // 2), score)  2.36 us

profile of v1, /device:TPU:1, one launch (start us, length us, event | category | flops | bytes accessed | tf_op | source)
XLA Modules:
  0.0 111.4 jit_solution(1541779600238998209)
XLA Ops:
  0.6 2.0 %copy.18 = bf16[8,8,2,2560]{3,1,2,0:T(8,128)(2,1)} copy(bf16[8,8,2,2560]{3,2,1,0:T(2,128)(2,1)} %bitcast.7) | data formatting | bytes 1310720
  2.6 1.4 %copy.15.req_ref = s32[64,1]{1,0:T(8,128)} copy(s32[64,1]{0,1:T(1,128)} %param.16) | data formatting | bytes 512 | tf_op args[3]
  4.0 1.3 %reshape.32.gain_ref = f32[1,2560]{1,0:T(1,128)} reshape(f32[2560]{0:T(1024)} %param.20) | data formatting | bytes 20480 | tf_op jit(solution)/shard_map/reshape | solution.py:518
  5.3 12.2 %qkv.1 = (bf16[1024,384]{1,0:T(8,128)(2,1)}, f32[512,384]{1,0:T(8,128)}, bf16[512,384]{1,0:T(8,128)(2,1)}, f32[4,64,384]{2,1,0:T(8,128)}) custom-call(bf16[64,5120]{1,0:T(8,128)(2,1)} %bitcast.5, s32[64,1]{1,0:T(8,128)} %copy.15.req_ref, s32[1,64]{1,0:T(1,128)} %bitcast.13, s32[1,48]{1,0:T(1,128)} %bitcast.11, s32[1,64]{1,0:T(1,128)} %bitcast.8, ...), custom_call_target="tpu_custom_call" | custom-call | tf_op jit(solution)/shard_map/qkv/pallas_call | solution.py:153
  17.5 21.5 %exchange0.1.q_ref = bf16[1024,384]{1,0:T(8,128)(2,1)} custom-call(bf16[1024,384]{1,0:T(8,128)(2,1)} %get-tuple-element.10.s_ref), custom_call_target="tpu_custom_call" | custom-call | tf_op jit(solution)/shard_map/exchange0/pallas_call | solution.py:220
  39.0 17.5 %slot.1.s_ref = bf16[1024,384]{1,0:T(8,128)(2,1)} custom-call(bf16[1024,384]{1,0:T(8,128)(2,1)} %exchange0.1.q_ref, bf16[1,4,2,80,2048]{4,3,2,1,0:T(8,128)(2,1)} %kv_ref.2, s32[1,64]{1,0:T(1,128)} %bitcast.9, s32[1,48]{1,0:T(1,128)} %bitcast.12), custom_call_target="tpu_custom_call" | custom-call | tf_op jit(solution)/shard_map/slot/pallas_call | solution.py:343
  56.4 16.8 %exchange1.1.b_ref = bf16[1024,384]{1,0:T(8,128)(2,1)} custom-call(bf16[1024,384]{1,0:T(8,128)(2,1)} %slot.1.s_ref), custom_call_target="tpu_custom_call" | custom-call | tf_op jit(solution)/shard_map/exchange1/pallas_call | solution.py:220
  73.2 13.4 %tail.1.t_ref = f32[512,384]{1,0:T(8,128)} custom-call(f32[512,384]{1,0:T(8,128)} %get-tuple-element.11.q_ref, bf16[64,4,2,80,256]{4,3,2,1,0:T(8,128)(2,1)} %kv_ref.3), custom_call_target="tpu_custom_call" | custom-call | tf_op jit(solution)/shard_map/tail/pallas_call | solution.py:283
  86.6 0.0 copy-start
  86.6 0.0 copy-start.1
  86.6 12.3 %mix.1 = (f32[128,2560]{1,0:T(8,128)}, bf16[128,2560]{1,0:T(8,128)(2,1)}) custom-call(bf16[1024,384]{1,0:T(8,128)(2,1)} %exchange1.1.b_ref, f32[512,384]{1,0:T(8,128)} %tail.1.t_ref, bf16[512,384]{1,0:T(8,128)(2,1)} %get-tuple-element.12.qb_ref, f32[4,64,384]{2,1,0:T(8,128)} %get-tuple-element.13.own_ref, s32[64,1]{1,0:T(8,128)} %copy.15.req_ref, ...), custom_call_target="tpu_custom_call" | custom-call | tf_op jit(solution)/shard_map/mix/pallas_call | solution.py:434
  99.0 0.0 copy-done
  99.0 0.6 reshape.33.gain_ref
  99.6 0.0 copy-done.1
  99.6 0.6 reshape.34.w_ref
  100.2 7.5 %finish.1 = (f32[64,2560]{1,0:T(8,128)}, f32[64,2]{1,0:T(8,128)}) custom-call(f32[128,2560]{1,0:T(8,128)} %get-tuple-element.14.m_ref, bf16[128,2560]{1,0:T(8,128)(2,1)} %get-tuple-element.15.mb_ref, bf16[64,5120]{1,0:T(8,128)(2,1)} %bitcast.6, f32[1,2560]{1,0:T(1,128)} %reshape.33.gain_ref, f32[1,2560]{1,0:T(1,128)} %reshape.34.w_ref), custom_call_target="tpu_custom_call" | custom-call | tf_op jit(solution)/shard_map/finish/pallas_call | solution.py:487
  107.7 2.4 %reshape.35 = f32[64,2,1280]{2,1,0:T(2,128)} reshape(f32[64,2560]{1,0:T(8,128)} %get-tuple-element.16) | data formatting | bytes 1310720 | tf_op jit(solution)/shard_map/reshape | solution.py:525
  110.1 1.4 %copy.17 = f32[64,2]{0,1:T(2,128)} copy(f32[64,2]{1,0:T(8,128)} %get-tuple-element.19) | data formatting | bytes 1024
Async XLA Ops:
  86.6 12.3 %copy-start = (f32[2560]{0:T(1024)S(1)}, f32[2560]{0:T(1024)}, u32[]{:S(2)}) copy-start(f32[2560]{0:T(1024)} %param.23) | copy-start | bytes 30724
  86.6 13.0 %copy-start.1 = (f32[2560]{0:T(1024)S(1)}, f32[2560]{0:T(1024)}, u32[]{:S(2)}) copy-start(f32[2560]{0:T(1024)} %param.24) | copy-start | bytes 30724

commit v2 on v1

--- a/solution.py
+++ b/solution.py
@@ -83,7 +83,7 @@
 
     @pl.when(step == last)
     def _():
-        req = req_ref[...].astype(F32)
+        req = to_col(req_ref[...].astype(F32), n)
         plen = plen_ref[...].astype(F32)
         reqs = plen.shape[1]
         slots = slot_ref.shape[1]
@@ -106,7 +106,7 @@
         for k in range(4):
             base = k * 6 * HD
             for j in range(4):
-                u = rope(acc[:, base + j * HD : base + (j + 1) * HD]).astype(BF16)
+                u = (rope(acc[:, base + j * HD : base + (j + 1) * HD]) * SCALE2).astype(BF16)
                 for t in range(2):
                     row = (t * 4 + j) * n
                     qb_ref[row : row + n, k * HD : (k + 1) * HD] = u[t * n : (t + 1) * n]
@@ -173,65 +173,6 @@
     )(x, req, tail, plen, slot, gain, freq, w)
 
 
-def exchange_kernel(groups, rows, s_ref, r_ref, send_sem, recv_sem, own_sem):
-    me = lax.axis_index("grp")
-    barrier = pltpu.get_barrier_semaphore()
-
-    def greet(d, _):
-        peer = lax.rem(me + d, groups)
-        pl.semaphore_signal(barrier, inc=1, device_id={"grp": peer}, device_id_type=MESH)
-        return 0
-
-    lax.fori_loop(1, groups, greet, 0)
-
-    def block(ref, i):
-        return ref.at[pl.ds(pl.multiple_of(i * rows, rows), rows)]
-
-    own = pltpu.make_async_copy(block(s_ref, me), block(r_ref, me), own_sem)
-    own.start()
-    pl.semaphore_wait(barrier, groups - 1)
-
-    def copy_to(d):
-        peer = lax.rem(me + d, groups)
-        return pltpu.make_async_remote_copy(
-            src_ref=block(s_ref, peer),
-            dst_ref=block(r_ref, me),
-            send_sem=send_sem.at[d],
-            recv_sem=recv_sem.at[d],
-            device_id={"grp": peer},
-            device_id_type=MESH,
-        )
-
-    def send(d, _):
-        copy_to(d).start()
-        return 0
-
-    def finish(d, _):
-        copy_to(d).wait()
-        return 0
-
-    lax.fori_loop(1, groups, send, 0)
-    lax.fori_loop(1, groups, finish, 0)
-    own.wait()
-
-
-def exchange(s, groups, number):
-    rows = s.shape[0] // groups
-    return pl.pallas_call(
-        functools.partial(exchange_kernel, groups, rows),
-        out_shape=jax.ShapeDtypeStruct(s.shape, s.dtype),
-        in_specs=[pl.BlockSpec(memory_space=pl.ANY)],
-        out_specs=pl.BlockSpec(memory_space=pl.ANY),
-        scratch_shapes=[
-            pltpu.SemaphoreType.DMA((groups,)),
-            pltpu.SemaphoreType.DMA((groups,)),
-            pltpu.SemaphoreType.DMA,
-        ],
-        compiler_params=pltpu.CompilerParams(collective_id=number, has_side_effects=True),
-        name="exchange" + str(number),
-    )(s)
-
-
 def store_side(ref, rows, logs):
     n = logs[0].shape[0]
     lane = iota((n, WIDE - SIDE), 1)
@@ -242,18 +183,18 @@
     ref[rows, SIDE:] = side.astype(ref.dtype)
 
 
-def tail_kernel(q_ref, kv_ref, o_ref):
+def tail_block(q_ref, kv_ref, o_ref, base):
     n = kv_ref.shape[0]
-    length = kv_ref.shape[4]
     scores = []
     limits = []
     for s in range(n):
-        limit = q_ref[s * 8 : (s + 1) * 8, SIDE : SIDE + 1]
+        rows = pl.ds(pl.multiple_of(base + s * 8, 8), 8)
+        limit = q_ref[rows, SIDE:][:, 0:1]
         for k in range(4):
-            q = q_ref[s * 8 : (s + 1) * 8, k * HD : (k + 1) * HD].astype(BF16)
+            q = q_ref[rows, k * HD : (k + 1) * HD].astype(BF16)
             scores.append(jnp.dot(q, kv_ref[s, k, 0], preferred_element_type=F32))
             limits.append(limit)
-    score = jnp.concatenate(scores, axis=0) * SCALE2
+    score = jnp.concatenate(scores, axis=0)
     limit = jnp.concatenate(limits, axis=0)
     at = iota(score.shape, 1).astype(F32)
     score = jnp.where(at < limit, score, NEG)
@@ -264,7 +205,7 @@
     logs = top + jnp.log2(total)
     weight = weight.astype(BF16)
     for s in range(n):
-        rows = slice(s * 8, (s + 1) * 8)
+        rows = pl.ds(pl.multiple_of(base + s * 8, 8), 8)
         parts = []
         for k in range(4):
             at = slice((s * 4 + k) * 8, (s * 4 + k + 1) * 8)
@@ -277,30 +218,89 @@
         store_side(o_ref, rows, parts)
 
 
-def tail_attention(qt, kv):
-    n = kv.shape[0]
-    step = 8
-    return pl.pallas_call(
-        tail_kernel,
-        grid=(n // step,),
-        in_specs=[
-            pl.BlockSpec((step * 8, WIDE), lambda i: (i, 0)),
-            pl.BlockSpec((step,) + kv.shape[1:], lambda i: (i, 0, 0, 0, 0)),
-        ],
-        out_specs=pl.BlockSpec((step * 8, WIDE), lambda i: (i, 0)),
-        out_shape=jax.ShapeDtypeStruct((n * 8, WIDE), F32),
-        compiler_params=pltpu.CompilerParams(vmem_limit_bytes=60 << 20),
-        name="tail",
-    )(qt, kv)
-
-
-def slot_kernel(q_ref, kv_ref, slot_ref, plen_ref, o_ref):
-    rows = q_ref.shape[0]
-    length = kv_ref.shape[4]
-    slots = slot_ref.shape[1]
+def core_kernel(
+    groups, rows, sub, qt_ref, slot_ref, plen_ref, s_ref, tail_hbm, slot_hbm,
+    t_ref, b_ref,
+    tail_buf, keys, values, got, out, tail_sem, slot_sem, send1, recv1, send2, recv2, own_sem,
+):
+    me = lax.axis_index("grp")
+    barrier = pltpu.get_barrier_semaphore()
+
+    def offset(i):
+        return lax.rem(i * 37, groups)
+
+    def ahead(i):
+        return lax.rem(me + offset(i), groups)
+
+    def behind(i):
+        return lax.rem(me + groups - offset(i), groups)
+
+    def greet(i, _):
+        pl.semaphore_signal(barrier, inc=1, device_id={"grp": ahead(i)}, device_id_type=MESH)
+        return 0
+
+    lax.fori_loop(1, groups, greet, 0)
+
+    def block(ref, i):
+        return ref.at[pl.ds(pl.multiple_of(i * rows, rows), rows)]
+
+    step = tail_buf.shape[1]
+    steps = tail_hbm.shape[0] // step
+
+    def fetch(i):
+        slot = lax.rem(i, 2)
+        return pltpu.make_async_copy(
+            tail_hbm.at[pl.ds(i * step, step)], tail_buf.at[slot], tail_sem.at[slot]
+        )
+
+    def tails(i):
+        fetch(i).wait()
+
+        @pl.when(i + 1 < steps)
+        def _():
+            fetch(i + 1).start()
+
+        tail_block(qt_ref, tail_buf.at[lax.rem(i, 2)], t_ref, i * (step * 8))
+
+    heads = keys.shape[0]
+    length = keys.shape[2]
+    caches = []
+    for k in range(heads):
+        caches.append(
+            pltpu.make_async_copy(slot_hbm.at[0, k, 0], keys.at[k, 0:HD], slot_sem.at[2 * k])
+        )
+        caches.append(
+            pltpu.make_async_copy(slot_hbm.at[0, k, 1], values.at[k, 0:HD], slot_sem.at[2 * k + 1])
+        )
+    fetch(0).start()
+    own_in = pltpu.make_async_copy(block(s_ref, me), block(got, 0), own_sem.at[0])
+    own_in.start()
+    tails(0)
+
+    def copy_out(i):
+        return pltpu.make_async_remote_copy(
+            src_ref=block(s_ref, ahead(i)), dst_ref=block(got, i),
+            send_sem=send1.at[i], recv_sem=recv1.at[i],
+            device_id={"grp": ahead(i)}, device_id_type=MESH,
+        )
+
+    def copy_back(i):
+        return pltpu.make_async_remote_copy(
+            src_ref=block(out, i), dst_ref=block(b_ref, me),
+            send_sem=send2.at[i], recv_sem=recv2.at[i],
+            device_id={"grp": behind(i)}, device_id_type=MESH,
+        )
+
+    def run(first, last, action):
+        def body(i, _):
+            action(i)
+            return 0
+
+        lax.fori_loop(first, last, body, 0)
+
+    slot = slot_ref[...].astype(F32)
+    slots = slot.shape[1]
     reqs = plen_ref.shape[1]
-    me = lax.axis_index("grp")
-    slot = slot_ref[...].astype(F32)
     at = iota((1, slots), 1)
     mine = jnp.sum(jnp.where(at == me, slot, 0.0), axis=1, keepdims=True)
     part = jnp.sum(jnp.where((slot == mine) & (at < me), 1.0, 0.0), axis=1, keepdims=True)
@@ -310,45 +310,98 @@
     start = part * float(length)
     index = iota((1, length), 1).astype(F32)
     bias = jnp.where(index < cached - start, 0.0, NEG)
-    sub = 128
+    more = keys.shape[1] - HD
+    first = iota((more, length), 0) == 0
+    for k in range(heads):
+        keys[k, HD:] = jnp.where(first, bias, 0.0).astype(BF16)
+        values[k, HD:] = jnp.where(first, 1.0, 0.0).astype(BF16)
+    floor0 = cached - float(W) - start
+
+    pl.semaphore_wait(barrier, groups - 1)
+    run(1, groups, lambda i: copy_out(i).start())
+    for copy in caches:
+        copy.start()
+
+    run(1, steps - 1, tails)
+    for copy in caches:
+        copy.wait()
+    own_in.wait()
     near = 384
-    for b in range(rows // sub):
-        span = slice(b * sub, (b + 1) * sub)
-        tail = q_ref[span, SIDE : SIDE + 128 - SIDE % 128].astype(F32)[:, 0:1]
+    per = sub // rows
+
+    def slot_block(b, _):
+        run(lax.max(b * per, 1), (b + 1) * per, lambda i: copy_out(i).wait_recv())
+        span = pl.ds(pl.multiple_of(b * sub, sub), sub)
+        tail = got[span, SIDE:].astype(F32)[:, 0:1]
         token = ((iota((sub, 1), 0) >> 2) & 1).astype(F32)
-        floor = tail + token + (cached - float(W)) - start
+        floor = tail + token + floor0
+        lane = iota((sub, 128), 1)
         logs = []
-        for k in range(4):
-            q = q_ref[span, k * HD : (k + 1) * HD]
-            score = jnp.dot(q, kv_ref[0, k, 0], preferred_element_type=F32)
-            score = score * SCALE2 + bias
+        for k in range(heads):
+            q = got[span, k * HD : k * HD + 128].astype(F32)
+            q = jnp.where(lane < HD, q, jnp.where(lane == HD, 1.0, 0.0)).astype(BF16)
+            score = jnp.dot(q, keys[k], preferred_element_type=F32)
             head = jnp.where(index[:, :near] > floor, score[:, :near], NEG)
             score = jnp.concatenate([head, score[:, near:]], axis=1)
             top = jnp.max(score, axis=1, keepdims=True)
-            weight = jnp.exp2(score - top)
-            total = jnp.sum(weight, axis=1, keepdims=True)
-            out = lax.dot_general(
-                weight.astype(BF16), kv_ref[0, k, 1], (((1,), (1,)), ((), ())),
-                preferred_element_type=F32,
+            weight = jnp.exp2(score - top).astype(BF16)
+            res = lax.dot_general(
+                weight, values[k], (((1,), (1,)), ((), ())), preferred_element_type=F32
             )
-            o_ref[span, k * HD : (k + 1) * HD] = (out * (1.0 / total)).astype(BF16)
+            total = res[:, HD : HD + 1]
+            out[span, k * HD : (k + 1) * HD] = (res[:, :HD] * (1.0 / total)).astype(BF16)
             logs.append(top + jnp.log2(total))
-        store_side(o_ref, span, logs)
-
-
-def slot_attention(r, kv, slot, plen):
-    rows = r.shape[0]
-    step = min(rows, 256)
-    full = lambda a: pl.BlockSpec(a.shape, lambda i: (0,) * a.ndim)
+        store_side(out, span, logs)
+
+        @pl.when(b > 0)
+        def _():
+            run(lax.max((b - 1) * per, 1), b * per, lambda i: copy_back(i).start())
+
+        return 0
+
+    blocks = groups // per
+    lax.fori_loop(0, blocks, slot_block, 0)
+    tails(steps - 1)
+    run(max((blocks - 1) * per, 1), groups, lambda i: copy_back(i).start())
+    own_out = pltpu.make_async_copy(block(out, 0), block(b_ref, me), own_sem.at[1])
+    own_out.start()
+    run(1, groups, lambda i: copy_out(i).wait_send())
+    run(1, groups, lambda i: copy_back(i).wait())
+    own_out.wait()
+
+
+def core(qt, slot, plen, send, tail_kv, slot_kv, groups):
+    rows = send.shape[0] // groups
+    sub = min(256, send.shape[0])
+    n = tail_kv.shape[0]
+    step = 8
+    heads = slot_kv.shape[1]
+    length = slot_kv.shape[4]
+    vmem = pl.BlockSpec(memory_space=pltpu.VMEM)
+    hbm = pl.BlockSpec(memory_space=pl.ANY)
+    dma = pltpu.SemaphoreType.DMA
     return pl.pallas_call(
-        slot_kernel,
-        grid=(rows // step,),
-        in_specs=[pl.BlockSpec((step, WIDE), lambda i: (i, 0)), full(kv), full(slot), full(plen)],
-        out_specs=pl.BlockSpec((step, WIDE), lambda i: (i, 0)),
-        out_shape=jax.ShapeDtypeStruct((rows, WIDE), BF16),
-        compiler_params=pltpu.CompilerParams(vmem_limit_bytes=60 << 20),
-        name="slot",
-    )(r, kv, slot, plen)
+        functools.partial(core_kernel, groups, rows, sub),
+        in_specs=[vmem, vmem, vmem, hbm, hbm, hbm],
+        out_specs=[vmem, hbm],
+        out_shape=[
+            jax.ShapeDtypeStruct((n * 8, WIDE), F32),
+            jax.ShapeDtypeStruct(send.shape, BF16),
+        ],
+        scratch_shapes=[
+            pltpu.VMEM((2, step) + tail_kv.shape[1:], BF16),
+            pltpu.VMEM((heads, 128, length), BF16),
+            pltpu.VMEM((heads, 128, length), BF16),
+            pltpu.VMEM(send.shape, BF16),
+            pltpu.VMEM(send.shape, BF16),
+            dma((2,)), dma((2 * heads,)),
+            dma((groups,)), dma((groups,)), dma((groups,)), dma((groups,)), dma((2,)),
+        ],
+        compiler_params=pltpu.CompilerParams(
+            collective_id=0, has_side_effects=True, vmem_limit_bytes=60 << 20
+        ),
+        name="core",
+    )(qt, slot, plen, send, tail_kv, slot_kv)
 
 
 def mix_kernel(b_ref, t_ref, qb_ref, own_ref, req_ref, slot_ref, wo_ref, m_ref, mb_ref, att):
@@ -358,7 +411,7 @@
         slots = slot_ref.shape[1]
         rows = 8 * n
         back = slots * 16
-        code = sample_codes(req_ref[...].astype(F32), 4.0, n)
+        code = sample_codes(to_col(req_ref[...].astype(F32), n), 4.0, n)
         spread = iota((rows, n), 1) == (iota((rows, n), 0) & (n - 1))
         code = jnp.sum(jnp.where(spread, to_row(code, n), 0.0), axis=1, keepdims=True)
         slot = slot_ref[...].astype(F32)
@@ -396,7 +449,7 @@
             s = jnp.dot(
                 query * keys, segment, preferred_element_type=F32,
                 precision=lax.Precision.HIGHEST,
-            ) * SCALE2
+            )
             if u:
                 s = jnp.where(iota(s.shape, 0) >= 4 * n, s, NEG)
             logs.append(s)
@@ -471,7 +524,7 @@
         )
         square = jnp.mean(total * total, axis=-1, keepdims=True)
         score = jnp.sum(total * scale, axis=-1, keepdims=True) * lax.rsqrt(square + EPS)
-        s_ref[:, t : t + 1] = score
+        s_ref[t : t + 1, :] = to_row(score, n)
         at = pl.multiple_of(tp * share + t * d, 128)
         h_ref[:, t * share : (t + 1) * share] = (
             x_ref[:, pl.ds(at, share)].astype(F32)
@@ -490,7 +543,7 @@
         out_specs=[vmem] * 2,
         out_shape=[
             jax.ShapeDtypeStruct((n, d), F32),
-            jax.ShapeDtypeStruct((n, 2), F32),
+            jax.ShapeDtypeStruct((2, n), F32),
         ],
         scratch_shapes=[
             pltpu.VMEM((2 * n, d), BF16),
@@ -515,14 +568,12 @@
     half = HD // 2
     freq = ROPE_BASE ** (-np.arange(half, dtype=np.float64) / half)
     freq = jnp.asarray(np.concatenate([freq, freq])[None, :], F32)
-    send, qt, qb, own = qkv(x, sample_req, tail, plen, slot, attn_gain.reshape(1, d), freq, wqkv)
-    got = exchange(send, groups, 0)
-    tails = tail_attention(qt, tail_kv)
-    part = slot_attention(got, slot_kv, slot, plen)
-    back = exchange(part, groups, 1)
-    m, mb = mix(back, tails, qb, own, sample_req, slot, wo)
+    req = sample_req.reshape(1, n)
+    send, qt, qb, own = qkv(x, req, tail, plen, slot, attn_gain.reshape(1, d), freq, wqkv)
+    tails, back = core(qt, slot, plen, send, tail_kv, slot_kv, groups)
+    m, mb = mix(back, tails, qb, own, req, slot, wo)
     h, score = finish(m, mb, x, out_gain.reshape(1, d), score_w.reshape(1, d))
-    return (h.reshape(n, 2, d // 2), score)
+    return (h.reshape(n, 2, d // 2), score.T)
 
 
 def solution(mesh):

time: 112 us -> 88.2 us (0.79)
  Pallas kernels: 101 us -> 78.8 us
  local copies, waits for them, and re-layouts: 9.62 us -> 8.12 us
    pallas_call x4 -> x1, Pallas kernels: 69.1 us -> 48.2 us  [core(): pl.pallas_call(functools.partial(core_kernel, groups, rows, sub), in_spec...]
    unnamed x7 -> x6, local copies, waits for them, and re-layouts: 4.75 us -> 3.23 us
    pallas_call x1, Pallas kernels: 7.51 us -> 6.17 us  [finish(): pl.pallas_call(finish_kernel, in_specs=[vmem] * 5, out_specs=[vmem] * 2,...]
where the time goes in v2:
time: 88.2 us; the launch traced here: 87.5 us
  Pallas kernels  78.8 us (89%)
  local copies, waits for them, and re-layouts  8.12 us (9%)
    pallas_call x1, Pallas kernels, core(): pl.pallas_call(functools.partial(core_kernel, groups, rows, sub), in_spec...  48.2 us
    pallas_call x1, Pallas kernels, mix(): pl.pallas_call(mix_kernel, grid=(d // width,), in_specs=[full(a) for a in...  12.2 us
    pallas_call x1, Pallas kernels, qkv(): pl.pallas_call(qkv_kernel, grid=(chunks,), in_specs=[full(a) for a in (x,...  12.1 us
    pallas_call x1, Pallas kernels, finish(): pl.pallas_call(finish_kernel, in_specs=[vmem] * 5, out_specs=[vmem] * 2,...  6.17 us
    unnamed x6, local copies, waits for them, and re-layouts  3.23 us
    reshape x1, local copies, waits for them, and re-layouts, local(): return (h.reshape(n, 2, d // 2), score.T)  2.36 us

profile of v2, /device:TPU:1, one launch (start us, length us, event | category | flops | bytes accessed | tf_op | source)
XLA Modules:
  0.0 87.5 jit_solution(259185858905899352)
XLA Ops:
  0.6 2.0 %copy.15 = bf16[8,8,2,2560]{3,1,2,0:T(8,128)(2,1)} copy(bf16[8,8,2,2560]{3,2,1,0:T(2,128)(2,1)} %bitcast.9) | data formatting | bytes 1310720
  2.6 1.3 %reshape.36.gain_ref = f32[1,2560]{1,0:T(1,128)} reshape(f32[2560]{0:T(1024)} %param.20) | data formatting | bytes 20480 | tf_op jit(solution)/shard_map/reshape | solution.py:572
  3.9 12.1 %qkv.1 = (bf16[1024,384]{1,0:T(8,128)(2,1)}, f32[512,384]{1,0:T(8,128)}, bf16[512,384]{1,0:T(8,128)(2,1)}, f32[4,64,384]{2,1,0:T(8,128)}) custom-call(bf16[64,5120]{1,0:T(8,128)(2,1)} %bitcast.7, s32[1,64]{1,0:T(1,128)} %bitcast.15, s32[1,64]{1,0:T(1,128)} %bitcast.18, s32[1,48]{1,0:T(1,128)} %bitcast.13, s32[1,64]{1,0:T(1,128)} %bitcast.10, ...), custom_call_target="tpu_custom_call" | custom-call | tf_op jit(solution)/shard_map/qkv/pallas_call | solution.py:153
  16.1 48.2 %core.1 = (f32[512,384]{1,0:T(8,128)}, bf16[1024,384]{1,0:T(8,128)(2,1)}) custom-call(f32[512,384]{1,0:T(8,128)} %get-tuple-element.12.qt_ref, s32[1,64]{1,0:T(1,128)} %bitcast.11, s32[1,48]{1,0:T(1,128)} %bitcast.14, bf16[1024,384]{1,0:T(8,128)(2,1)} %get-tuple-element.13.s_ref, bf16[64,4,2,80,256]{4,3,2,1,0:T(8,128)(2,1)} %tail_hbm.1, ...), custom_call_target="tpu_custom_call" | custom-call | tf_op jit(solution)/shard_map/core/pallas_call | solution.py:383
  64.3 0.0 copy-start
  64.3 0.0 copy-start.1
  64.3 12.2 %mix.1 = (f32[128,2560]{1,0:T(8,128)}, bf16[128,2560]{1,0:T(8,128)(2,1)}) custom-call(bf16[1024,384]{1,0:T(8,128)(2,1)} %get-tuple-element.14.b_ref, f32[512,384]{1,0:T(8,128)} %get-tuple-element.15.t_ref, bf16[512,384]{1,0:T(8,128)(2,1)} %get-tuple-element.16.qb_ref, f32[4,64,384]{2,1,0:T(8,128)} %get-tuple-element.17.own_ref, s32[1,64]{1,0:T(1,128)} %bitcast.16, ...), custom_call_target="tpu_custom_call" | custom-call | tf_op jit(solution)/shard_map/mix/pallas_call | solution.py:487
  76.6 0.0 copy-done
  76.6 0.6 reshape.37.gain_ref
  77.2 0.0 copy-done.1
  77.2 0.6 reshape.38.w_ref
  77.8 6.2 %finish.1 = (f32[64,2560]{1,0:T(8,128)}, f32[2,64]{1,0:T(2,128)}) custom-call(f32[128,2560]{1,0:T(8,128)} %get-tuple-element.18.m_ref, bf16[128,2560]{1,0:T(8,128)(2,1)} %get-tuple-element.19.mb_ref, bf16[64,5120]{1,0:T(8,128)(2,1)} %bitcast.8, f32[1,2560]{1,0:T(1,128)} %reshape.37.gain_ref, f32[1,2560]{1,0:T(1,128)} %reshape.38.w_ref), custom_call_target="tpu_custom_call" | custom-call | tf_op jit(solution)/shard_map/finish/pallas_call | solution.py:540
  84.0 2.4 %reshape.39 = f32[64,2,1280]{2,1,0:T(2,128)} reshape(f32[64,2560]{1,0:T(8,128)} %get-tuple-element.20) | data formatting | bytes 1310720 | tf_op jit(solution)/shard_map/reshape | solution.py:576
  86.3 1.2 %copy.17 = f32[64,2]{0,1:T(2,128)} copy(f32[64,2]{0,1:T(2,128)} %bitcast.17) | data formatting | bytes 1024
Async XLA Ops:
  64.3 12.3 %copy-start = (f32[2560]{0:T(1024)S(1)}, f32[2560]{0:T(1024)}, u32[]{:S(2)}) copy-start(f32[2560]{0:T(1024)} %param.23) | copy-start | bytes 30724
  64.3 12.9 %copy-start.1 = (f32[2560]{0:T(1024)S(1)}, f32[2560]{0:T(1024)}, u32[]{:S(2)}) copy-start(f32[2560]{0:T(1024)} %param.24) | copy-start | bytes 30724

commit v3 on v2

v3 whole, which is shorter than its diff:
```python
import functools

import jax
import jax.numpy as jnp
import numpy as np
from jax import lax
from jax.experimental import pallas as pl
from jax.experimental.pallas import tpu as pltpu
from jax.sharding import PartitionSpec as P

W = 4096
HD = 80
EPS = 1e-05
ROPE_BASE = 10000.0
NEG = -1e30
MESH = pl.DeviceIdType.MESH
F32 = jnp.float32
BF16 = jnp.bfloat16
LOG2E = 1.4426950408889634
SCALE2 = HD**-0.5 * LOG2E
WIDE = 384
SIDE = 320


def iota(shape, dim):
    return lax.broadcasted_iota(jnp.int32, shape, dim)


def to_row(col, size):
    eye = iota((size, size), 0) == iota((size, size), 1)
    return jnp.sum(jnp.where(eye, col, 0.0), axis=0, keepdims=True)


def to_col(row, size):
    eye = iota((size, size), 0) == iota((size, size), 1)
    return jnp.sum(jnp.where(eye, row, 0.0), axis=1, keepdims=True)


def as_row(ref):
    return jnp.concatenate([ref[c : c + 1, :] for c in range(ref.shape[0])], axis=1)


def put(ref, tj, value):
    for c in range(ref.shape[0]):
        ref[c, pl.ds(tj, value.shape[0], stride=8), :] = value[:, c * 128 : (c + 1) * 128]


def take(ref, tj):
    count = ref.shape[1] // 8
    return jnp.concatenate(
        [ref[c, pl.ds(tj, count, stride=8), :] for c in range(ref.shape[0])], axis=1
    )


def joined(ref, rows):
    return jnp.concatenate([ref[c, rows, :] for c in range(ref.shape[0])], axis=1)


def split3(x):
    hi = x.astype(BF16).astype(F32)
    rest = x - hi
    mid = rest.astype(BF16).astype(F32)
    low = (rest - mid).astype(BF16).astype(F32)
    return hi, mid, low


def sample_codes(req, rank_scale, samples):
    req_row = to_row(req, samples)
    shape = (samples, samples)
    before = (req == req_row) & (iota(shape, 1) < iota(shape, 0))
    rank = jnp.sum(jnp.where(before, 1.0, 0.0), axis=1, keepdims=True)
    return req * rank_scale + rank


def store_side(ref, rows, logs):
    n = logs[0].shape[0]
    lane = iota((n, WIDE - SIDE), 1)
    side = jnp.where(lane == 12, 1.0, 0.0)
    for k, value in enumerate(logs):
        for p, term in enumerate(split3(value)):
            side = jnp.where(lane == 4 * p + k, term, side)
    ref[rows, SIDE:] = side.astype(ref.dtype)


def tail_block(q_ref, kv_ref, o_ref, base):
    n = kv_ref.shape[0]
    scores = []
    limits = []
    for s in range(n):
        rows = pl.ds(pl.multiple_of(base + s * 8, 8), 8)
        packed = joined(q_ref, rows)
        limit = packed[:, SIDE : SIDE + 1]
        for k in range(4):
            q = packed[:, k * HD : (k + 1) * HD].astype(BF16)
            scores.append(jnp.dot(q, kv_ref[s, k, 0], preferred_element_type=F32))
            limits.append(limit)
    score = jnp.concatenate(scores, axis=0)
    limit = jnp.concatenate(limits, axis=0)
    at = iota(score.shape, 1).astype(F32)
    score = jnp.where(at < limit, score, NEG)
    top = jnp.max(score, axis=1, keepdims=True)
    weight = jnp.exp2(score - top)
    total = jnp.sum(weight, axis=1, keepdims=True)
    inverse = 1.0 / total
    logs = top + jnp.log2(total)
    weight = weight.astype(BF16)
    for s in range(n):
        rows = pl.ds(pl.multiple_of(base + s * 8, 8), 8)
        parts = []
        outs = []
        for k in range(4):
            at = slice((s * 4 + k) * 8, (s * 4 + k + 1) * 8)
            out = lax.dot_general(
                weight[at], kv_ref[s, k, 1], (((1,), (1,)), ((), ())),
                preferred_element_type=F32,
            )
            outs.append(out * inverse[at])
            parts.append(logs[at])
        lane = iota((8, WIDE - SIDE), 1)
        side = jnp.zeros((8, WIDE - SIDE), F32)
        for k in range(4):
            side = jnp.where(lane == k, parts[k], side)
        value = jnp.concatenate(outs + [side], axis=1)
        for c in range(o_ref.shape[0]):
            o_ref[c, rows, :] = value[:, c * 128 : (c + 1) * 128]


def core_kernel(
    groups, rows, sub, x_ref, req_ref, len_ref, slot_ref, plen_ref, gain_ref, freq_ref,
    wqkv_hbm, tail_hbm, slot_hbm, wo_hbm,
    m_ref, g_ref,
    wqkv, normed, xt, turn, acc, qt_ref, qb_ref, own_ref, s_ref,
    t_ref, b_ref, tail_buf, keys, values, got, out, wo, wide, own_log, home, att, mb,
    tail_sem, slot_sem, send1, recv1, send2, recv2, own_sem, wo_sem, send3, recv3, wq_sem,
):
    me = lax.axis_index("grp")
    barrier = pltpu.get_barrier_semaphore()
    pieces, deep, _ = wqkv.shape

    def project_copy(c):
        at = pl.multiple_of(c * deep, deep)
        return pltpu.make_async_copy(wqkv_hbm.at[pl.ds(at, deep)], wqkv.at[c], wq_sem.at[c])

    for c in range(pieces):
        project_copy(c).start()

    def offset(i):
        return lax.rem(i * 37, groups)

    def ahead(i):
        return lax.rem(me + offset(i), groups)

    def behind(i):
        return lax.rem(me + groups - offset(i), groups)

    def greet(i, _):
        pl.semaphore_signal(barrier, inc=1, device_id={"grp": ahead(i)}, device_id_type=MESH)
        return 0

    lax.fori_loop(1, groups, greet, 0)
    partner = {"tp": 1 - lax.axis_index("tp")}
    pl.semaphore_signal(barrier, inc=1, device_id=partner, device_id_type=MESH)

    def block(ref, i):
        return ref.at[pl.ds(pl.multiple_of(i * rows, rows), rows)]

    step = tail_buf.shape[1]
    steps = tail_hbm.shape[0] // step
    depth = tail_buf.shape[0]
    heads = keys.shape[0]
    length = keys.shape[2]

    def fetch(i):
        slot = lax.rem(i, depth)
        return pltpu.make_async_copy(
            tail_hbm.at[pl.ds(i * step, step)], tail_buf.at[slot], tail_sem.at[slot]
        )

    def tails(i):
        fetch(i).wait()

        @pl.when(i + depth - 1 < steps)
        def _():
            fetch(i + depth - 1).start()

        tail_block(qt_ref, tail_buf.at[lax.rem(i, depth)], t_ref, i * (step * 8))

    caches = []
    for k in range(heads):
        caches.append(
            pltpu.make_async_copy(slot_hbm.at[0, k, 0], keys.at[k, 0:HD], slot_sem.at[2 * k])
        )
        caches.append(
            pltpu.make_async_copy(slot_hbm.at[0, k, 1], values.at[k, 0:HD], slot_sem.at[2 * k + 1])
        )
    n = x_ref.shape[0]
    for t in range(2):
        at = slice(t * n, (t + 1) * n)
        x = x_ref[:, t, :].astype(F32)
        xt[at, :] = x.astype(BF16)
        r = lax.rsqrt(jnp.mean(x * x, axis=-1, keepdims=True) + EPS)
        y = (x * r * as_row(gain_ref)).astype(BF16)
        for c in range(pieces):
            normed[c, at, :] = y[:, c * deep : (c + 1) * deep]
    req = to_col(req_ref[...].astype(F32), n)
    plen = plen_ref[...].astype(F32)
    slot = slot_ref[...].astype(F32)
    slots = slot.shape[1]
    reqs = plen.shape[1]
    owned = req == iota((n, reqs), 1).astype(F32)
    tail = to_col(len_ref[...].astype(F32), n)
    pos = jnp.sum(jnp.where(owned, plen, 0.0), axis=1, keepdims=True) + tail
    angle = jnp.concatenate([pos, pos + 1.0], axis=0) * freq_ref[...]
    half = HD // 2
    sine = jnp.sin(angle)
    turn[0] = jnp.cos(angle)
    turn[1] = jnp.where(iota(sine.shape, 1) < half, -sine, sine)
    acc[...] = jnp.zeros_like(acc)
    own_ref[...] = jnp.zeros_like(own_ref)

    def project(c, _):
        project_copy(c).wait()
        acc[...] += jnp.dot(normed[c], wqkv[c], preferred_element_type=F32)
        return 0

    lax.fori_loop(0, pieces, project, 0)
    for i in range(depth - 1):
        fetch(i).start()

    def rope(u):
        turned = jnp.concatenate([u[:, half:], u[:, :half]], axis=1)
        return u * turn[0] + turned * turn[1]

    for k in range(heads):
        base = k * 6 * HD
        for j in range(4):
            u = (rope(acc[:, base + j * HD : base + (j + 1) * HD]) * SCALE2).astype(BF16)
            for t in range(2):
                row = (t * 4 + j) * n
                qb_ref[row : row + n, k * HD : (k + 1) * HD] = u[t * n : (t + 1) * n]
        fresh = rope(acc[:, base + 4 * HD : base + 5 * HD]).astype(BF16).astype(F32)
        value = acc[:, base + 5 * HD : base + 6 * HD].astype(BF16).astype(F32)
        for t in range(2):
            own_ref[t, :, k * HD : (k + 1) * HD] = fresh[t * n : (t + 1) * n]
            own_ref[2 + t, :, k * HD : (k + 1) * HD] = value[t * n : (t + 1) * n]
    side = jnp.broadcast_to(tail, (n, WIDE - SIDE)).astype(BF16)
    code = to_row(sample_codes(req, 2.0, n), n)
    spread = iota((2 * slots, slots), 1) == (iota((2 * slots, slots), 0) >> 1)
    want = jnp.sum(jnp.where(spread, slot, 0.0), axis=1, keepdims=True) * 2.0
    want = want + (iota((2 * slots, 1), 0) & 1).astype(F32)
    pick = jnp.where(want == code, 1.0, 0.0).astype(BF16)
    for tj in range(8):
        at = slice(tj * n, (tj + 1) * n)
        qb_ref[at, SIDE:] = side
        q = qb_ref[at, :]
        put(qt_ref, tj, q.astype(F32))
        put(wide, tj, jnp.dot(pick, q, preferred_element_type=F32))
    for c in range(3):
        s_ref[:, c * 128 : (c + 1) * 128] = wide[c].astype(BF16)
    own_in = pltpu.make_async_copy(block(s_ref, me), block(got, 0), own_sem.at[0])
    tails(0)

    def copy_out(i):
        return pltpu.make_async_remote_copy(
            src_ref=block(s_ref, ahead(i)), dst_ref=block(got, i),
            send_sem=send1.at[i], recv_sem=recv1.at[i],
            device_id={"grp": ahead(i)}, device_id_type=MESH,
        )

    def copy_back(i):
        return pltpu.make_async_remote_copy(
            src_ref=block(out, i), dst_ref=block(b_ref, me),
            send_sem=send2.at[i], recv_sem=recv2.at[i],
            device_id={"grp": behind(i)}, device_id_type=MESH,
        )

    def run(first, last, action):
        def body(i, _):
            action(i)
            return 0

        lax.fori_loop(first, last, body, 0)

    at = iota((1, slots), 1)
    mine = jnp.sum(jnp.where(at == me, slot, 0.0), axis=1, keepdims=True)
    part = jnp.sum(jnp.where((slot == mine) & (at < me), 1.0, 0.0), axis=1, keepdims=True)
    owned = iota((1, reqs), 1).astype(F32) == mine
    tokens = jnp.sum(jnp.where(owned, plen, 0.0), axis=1, keepdims=True)
    cached = jnp.minimum(tokens, float(W))
    start = part * float(length)
    index = iota((1, length), 1).astype(F32)
    bias = jnp.where(index < cached - start, 0.0, NEG)
    more = keys.shape[1] - HD
    first = iota((more, length), 0) == 0
    for k in range(heads):
        keys[k, HD:] = jnp.where(first, bias, 0.0).astype(BF16)
        values[k, HD:] = jnp.where(first, 1.0, 0.0).astype(BF16)
    floor0 = cached - float(W) - start

    pl.semaphore_wait(barrier, groups)
    own_in.start()
    run(1, groups, lambda i: copy_out(i).start())
    for copy in caches:
        copy.start()

    run(1, steps - 1, tails)
    chunks, _, width = wo.shape
    weights = [
        pltpu.make_async_copy(wo_hbm.at[:, c * width : (c + 1) * width], wo.at[c], wo_sem.at[c])
        for c in range(chunks)
    ]
    for copy in weights:
        copy.start()
    shape = (WIDE, WIDE)
    head_of = iota(shape, 1) // HD
    segment = jnp.where((iota(shape, 0) // HD == head_of) & (head_of < heads), 1.0, 0.0)
    segment = segment.astype(BF16)
    for tj in range(8):
        at = slice(tj * n, (tj + 1) * n)
        query = qb_ref[at, :].astype(F32)
        for u in range(2 if tj >= 4 else 1):
            prod = query * own_ref[u]
            high = prod.astype(BF16)
            low = (prod - high.astype(F32)).astype(BF16)
            own_log[u, at, :] = jnp.dot(high, segment, preferred_element_type=F32) + jnp.dot(
                low, segment, preferred_element_type=F32
            )
    shape = (128, WIDE)
    lane = iota(shape, 0) - (SIDE - 256)
    head_of = iota(shape, 1) // HD
    one_term = jnp.where((lane == head_of) & (head_of < heads), 1.0, 0.0).astype(BF16)
    same = (lane >= 0) & (lane < 12) & ((lane & 3) == head_of)
    terms = jnp.where(same, 1.0, 0.0).astype(BF16)
    code = sample_codes(req, 4.0, n)
    slot_col = to_col(slot, slots)
    earlier = (slot == slot_col) & (iota((slots, slots), 1) < iota((slots, slots), 0))
    key = jnp.sum(jnp.where(earlier, 1.0, 0.0), axis=1, keepdims=True) * 2.0 + slot_col * 4.0
    spread = iota((slots, 2 * slots), 0) == (iota((slots, 2 * slots), 1) >> 1)
    key = jnp.sum(jnp.where(spread, key, 0.0), axis=0, keepdims=True)
    key = key + (iota((1, 2 * slots), 1) & 1).astype(F32)
    code = jnp.concatenate([code, code + 2.0], axis=0)
    pick = jnp.where(key == code, 1.0, 0.0)
    split = jnp.sum(pick[n:], axis=1, keepdims=True) > 0.5
    pick = pick.astype(BF16)
    for copy in caches:
        copy.wait()
    own_in.wait()
    near = 384
    per = sub // rows

    def slot_block(b, _):
        run(lax.max(b * per, 1), (b + 1) * per, lambda i: copy_out(i).wait_recv())
        for h in range(2):
            span = pl.ds(pl.multiple_of(b * sub + h * (sub // 2), sub // 2), sub // 2)
            tail = got[span, SIDE:].astype(F32)[:, 0:1]
            token = ((iota((sub // 2, 1), 0) >> 2) & 1).astype(F32)
            floor = tail + token + floor0
            lane = iota((sub // 2, 96), 1)
            logs = []
            for k in range(heads):
                q = got[span, k * HD : k * HD + 96].astype(F32)
                q = jnp.where(lane < HD, q, jnp.where(lane == HD, 1.0, 0.0)).astype(BF16)
                score = jnp.dot(q, keys[k], preferred_element_type=F32)
                head = jnp.where(index[:, :near] > floor, score[:, :near], NEG)
                score = jnp.concatenate([head, score[:, near:]], axis=1)
                top = jnp.max(score, axis=1, keepdims=True)
                weight = jnp.exp2(score - top).astype(BF16)
                res = lax.dot_general(
                    weight, values[k], (((1,), (1,)), ((), ())), preferred_element_type=F32
                )
                total = res[:, HD : HD + 1]
                out[span, k * HD : (k + 1) * HD] = (res[:, :HD] * (1.0 / total)).astype(BF16)
                logs.append(top + jnp.log2(total))
            store_side(out, span, logs)

        @pl.when(b > 0)
        def _():
            run(lax.max((b - 1) * per, 1), b * per, lambda i: copy_back(i).start())

        return 0

    blocks = groups // per
    lax.fori_loop(0, blocks, slot_block, 0)
    tails(steps - 1)
    run(max((blocks - 1) * per, 1), groups, lambda i: copy_back(i).start())
    own_out = pltpu.make_async_copy(block(out, 0), block(b_ref, me), own_sem.at[1])
    own_out.start()

    for tj in range(8):
        at = slice(tj * n, (tj + 1) * n)
        tail = take(t_ref, tj)
        spread = [
            jnp.dot(x.astype(BF16), one_term, preferred_element_type=F32)
            for x in split3(tail[:, 256:])
        ]
        logs = [functools.reduce(jnp.add, spread), own_log[0, at, :]]
        parts = [tail, own_ref[2]]
        if tj >= 4:
            logs.append(own_log[1, at, :])
            parts.append(own_ref[3])
        top = functools.reduce(jnp.maximum, logs)
        shares = [jnp.exp2(x - top) for x in logs]
        home[at, :] = functools.reduce(jnp.add, [w * v for w, v in zip(shares, parts)])
        own_log[0, at, :] = top
        own_log[1, at, :] = functools.reduce(jnp.add, shares)

    run(1, groups, lambda i: copy_back(i).wait_recv())
    own_out.wait()
    for c in range(3):
        wide[c] = b_ref[:, c * 128 : (c + 1) * 128].astype(F32)
    for tj in range(8):
        at = slice(tj * n, (tj + 1) * n)
        both = jnp.dot(pick, take(wide, tj).astype(BF16), preferred_element_type=F32)
        logs = jnp.dot(both[:, 256:].astype(BF16), terms, preferred_element_type=F32)
        log1 = logs[:n]
        log2 = jnp.where(split, logs[n:], NEG)
        top = own_log[0, at, :]
        peak = jnp.maximum(top, jnp.maximum(log1, log2))
        w0 = jnp.exp2(top - peak)
        w1 = jnp.exp2(log1 - peak)
        w2 = jnp.exp2(log2 - peak)
        res = home[at, :] * w0 + both[:n] * w1 + both[n:] * w2
        res = (res * (1.0 / (own_log[1, at, :] * w0 + w1 + w2))).astype(BF16)
        t, j = divmod(tj, 4)
        for k in range(heads):
            att[t * n : (t + 1) * n, (k * 4 + j) * HD : (k * 4 + j + 1) * HD] = res[
                :, k * HD : (k + 1) * HD
            ]

    def give(c):
        cols = slice(c * width, (c + 1) * width)
        return pltpu.make_async_remote_copy(
            src_ref=mb.at[:, cols], dst_ref=g_ref.at[:, cols],
            send_sem=send3.at[c], recv_sem=recv3.at[c],
            device_id=partner, device_id_type=MESH,
        )

    for c in range(chunks):
        weights[c].wait()
        mixed = jnp.dot(att[...], wo[c], preferred_element_type=F32)
        cols = slice(c * width, (c + 1) * width)
        m_ref[:, cols] = mixed + xt[:, cols].astype(F32)
        mb[:, c * width : (c + 1) * width] = mixed.astype(BF16)
        if c:
            give(c - 1).start()
    run(1, groups, lambda i: copy_out(i).wait_send())
    run(1, groups, lambda i: copy_back(i).wait_send())
    give(chunks - 1).start()
    for c in range(chunks):
        give(c).wait()


def core(x, req, tail, slot, plen, gain, freq, wqkv, tail_kv, slot_kv, wo, groups):
    n = tail_kv.shape[0]
    rows = 16
    send = jax.ShapeDtypeStruct((groups * rows, WIDE), BF16)
    sub = min(256, groups * rows)
    step = 8
    heads = slot_kv.shape[1]
    length = slot_kv.shape[4]
    depth, d = wo.shape
    chunks = 5
    vmem = pl.BlockSpec(memory_space=pltpu.VMEM)
    hbm = pl.BlockSpec(memory_space=pl.ANY)
    dma = pltpu.SemaphoreType.DMA
    return pl.pallas_call(
        functools.partial(core_kernel, groups, rows, sub),
        in_specs=[vmem] * 7 + [hbm] * 4,
        out_specs=[vmem, hbm],
        out_shape=[
            jax.ShapeDtypeStruct((2 * n, d), F32),
            jax.ShapeDtypeStruct((2 * n, d), BF16),
        ],
        scratch_shapes=[
            pltpu.VMEM((chunks, d // chunks, wqkv.shape[1]), BF16),
            pltpu.VMEM((chunks, 2 * n, d // chunks), BF16),
            pltpu.VMEM((2 * n, d), BF16),
            pltpu.VMEM((2, 2 * n, HD), F32),
            pltpu.VMEM((2 * n, wqkv.shape[1]), F32),
            pltpu.VMEM((3, n * 8, 128), F32),
            pltpu.VMEM((n * 8, WIDE), BF16),
            pltpu.VMEM((4, n, WIDE), F32),
            pltpu.VMEM(send.shape, BF16),
            pltpu.VMEM((3, n * 8, 128), F32),
            pltpu.VMEM(send.shape, BF16),
            pltpu.VMEM((4, step) + tail_kv.shape[1:], BF16),
            pltpu.VMEM((heads, 96, length), BF16),
            pltpu.VMEM((heads, 96, length), BF16),
            pltpu.VMEM(send.shape, BF16),
            pltpu.VMEM(send.shape, BF16),
            pltpu.VMEM((chunks, depth, d // chunks), BF16),
            pltpu.VMEM((3, send.shape[0], 128), F32),
            pltpu.VMEM((2, n * 8, WIDE), F32),
            pltpu.VMEM((n * 8, WIDE), F32),
            pltpu.VMEM((2 * n, depth), BF16),
            pltpu.VMEM((2 * n, d), BF16),
            dma((4,)), dma((2 * heads,)),
            dma((groups,)), dma((groups,)), dma((groups,)), dma((groups,)), dma((2,)),
            dma((chunks,)), dma((chunks,)), dma((chunks,)), dma((chunks,)),
        ],
        compiler_params=pltpu.CompilerParams(
            collective_id=0, has_side_effects=True, vmem_limit_bytes=60 << 20
        ),
        name="core",
    )(x, req, tail, slot, plen, gain, freq, wqkv, tail_kv, slot_kv, wo)


def finish_kernel(m_ref, g_ref, gain_ref, w_ref, h_ref, s_ref):
    n = m_ref.shape[0] // 2
    d = m_ref.shape[1]
    share = d // 2
    tp = lax.axis_index("tp")
    scale = as_row(gain_ref) * as_row(w_ref)
    mine = pl.multiple_of(tp * share, 128)
    for t in range(2):
        rows = slice(t * n, (t + 1) * n)
        total = m_ref[rows, :] + g_ref[rows, :].astype(F32)
        square = jnp.mean(total * total, axis=-1, keepdims=True)
        score = jnp.sum(total * scale, axis=-1, keepdims=True) * lax.rsqrt(square + EPS)
        s_ref[t : t + 1, :] = to_row(score, n)
        h_ref[:, t, :] = m_ref[rows, pl.ds(mine, share)] + g_ref[rows, pl.ds(mine, share)].astype(F32)


def finish(m, g, gain, w):
    n = m.shape[0] // 2
    d = m.shape[1]
    vmem = pl.BlockSpec(memory_space=pltpu.VMEM)
    return pl.pallas_call(
        finish_kernel,
        in_specs=[vmem] * 4,
        out_specs=[vmem] * 2,
        out_shape=[
            jax.ShapeDtypeStruct((n, 2, d // 2), F32),
            jax.ShapeDtypeStruct((2, n), F32),
        ],
        name="finish",
    )(m, g, gain, w)


def local(
    hidden_in, prompt_len, slot_req, sample_req, tail_len, slot_kv, tail_kv,
    attn_gain, wqkv, wo, out_gain, score_w,
):
    n, _, d = hidden_in.shape
    groups = lax.axis_size("grp")
    tail = tail_len.reshape(1, n)
    plen = prompt_len.reshape(1, -1)
    slot = slot_req.reshape(1, -1)
    half = HD // 2
    freq = ROPE_BASE ** (-np.arange(half, dtype=np.float64) / half)
    freq = jnp.asarray(np.concatenate([freq, freq])[None, :], F32)
    req = sample_req.reshape(1, n)
    req = sample_req.reshape(1, n)
    fold = lambda v: v.reshape(d // 128, 128)
    m, g = core(
        hidden_in, req, tail, slot, plen, fold(attn_gain), freq,
        wqkv, tail_kv, slot_kv, wo, groups,
    )
    h, score = finish(m, g, fold(out_gain), fold(score_w))
    return (h, score.T)


def solution(mesh):
    in_specs = (
        P("grp", None, None),
        P(),
        P(),
        P("grp", None),
        P("grp"),
        P("grp", "tp", None, None, None),
        P("grp", "tp", None, None, None),
        P(),
        P(None, "tp"),
        P("tp", None),
        P(),
        P(),
    )
    out_specs = (P("grp", None, "tp"), P("grp", None))
    return jax.shard_map(local, mesh=mesh, in_specs=in_specs, out_specs=out_specs, check_vma=False)
```

time: 88.2 us -> 63.3 us (0.72)
  Pallas kernels: 78.8 us -> 62.5 us
  local copies, waits for them, and re-layouts: 8.12 us -> 0 us
    pallas_call x3 -> x1, Pallas kernels: 30.6 us -> 2.86 us  [finish(): pl.pallas_call(finish_kernel, in_specs=[vmem] * 4, out_specs=[vmem] * 2,...]
    pallas_call x1, Pallas kernels: 48.2 us -> 59.6 us  [core(): pl.pallas_call(functools.partial(core_kernel, groups, rows, sub), in_spec...]
    reshape x4 -> x0, local copies, waits for them, and re-layouts: 4.89 us -> none  [the longest x1 2.36 us: local(): return (h.reshape(n, 2, d // 2), score.T)]
    unnamed x6 -> x0, local copies, waits for them, and re-layouts: 3.23 us -> none
where the time goes in v3:
time: 63.3 us; the launch traced here: 63.1 us
  Pallas kernels  62.5 us (99%)
  between operations  0.64 us (1%)
    pallas_call x1, Pallas kernels, core(): pl.pallas_call(functools.partial(core_kernel, groups, rows, sub), in_spec...  59.6 us
    pallas_call x1, Pallas kernels, finish(): pl.pallas_call(finish_kernel, in_specs=[vmem] * 4, out_specs=[vmem] * 2,...  2.86 us

profile of v3, /device:TPU:1, one launch (start us, length us, event | category | flops | bytes accessed | tf_op | source)
XLA Modules:
  0.0 63.1 jit_solution(15758753074945404503)
XLA Ops:
  0.6 59.6 %core.1 = (f32[128,2560]{1,0:T(8,128)}, bf16[128,2560]{1,0:T(8,128)(2,1)}) custom-call(bf16[64,2,2560]{2,1,0:T(2,128)(2,1)} %x_ref.1, s32[1,64]{1,0:T(1,128)} %bitcast.11, s32[1,64]{1,0:T(1,128)} %bitcast.12, s32[1,64]{1,0:T(1,128)} %bitcast.13, s32[1,48]{1,0:T(1,128)} %bitcast.14, f32[20,128]{1,0:T(8,128)} %bitcast.8, f32[1,80]{1,0:T(1,128)} %constant.2.clone.freq_ref, ...), custom_call_target="tpu_custom_call" | custom-call | tf_op jit(solution)/shard_map/core/pallas_call | solution.py:466
  60.2 2.9 %finish.1 = (f32[64,2,1280]{2,1,0:T(2,128)}, f32[2,64]{1,0:T(2,128)}) custom-call(f32[128,2560]{1,0:T(8,128)} %get-tuple-element.6.m_ref, bf16[128,2560]{1,0:T(8,128)(2,1)} %get-tuple-element.7.g_ref, f32[20,128]{1,0:T(8,128)} %bitcast.9, f32[20,128]{1,0:T(8,128)} %bitcast.10), custom_call_target="tpu_custom_call" | custom-call | tf_op jit(solution)/shard_map/finish/pallas_call | solution.py:528
